TPU v7x, 32 devices: a whole 2x2x4 slice. The times are simulated.
32 devices in a mesh: seq: 16 (over z, x, core), head: 2 (over y).
Axes of the slice: x: 2, y: 2, z: 4, core: 2. Of those that a mesh axis runs over, the one named last changes fastest.
Arguments:
- byte_rows: bfloat16 [16384, 1024], P('seq', 'head'), may hold values from -6 to 6
- pool_weight: bfloat16 [4, 1024, 1024], P(None, 'head'), may hold values from -0.09375 to 0.09375
- norm_gain: float32 [1024], replicated, may hold values from 0.1 to 1.9
- qkv_weight: bfloat16 [1024, 8, 3, 128], P(None, 'head')
- span_order: int32 [16], replicated, may hold values from 0 to 15, as said below
- query_start: int32 [1], replicated, may hold values from 2560 to 3072
Outputs:
- shortened: bfloat16 [4096, 1024], P('seq', 'head')
- context: bfloat16 [1024, 1024], P('seq', 'head')
- row_highest: float32 [8, 1024], P('head', 'seq')
Inputs may be any that keep to these rules, and one draw needn't show every extreme that they name: `span_order`: entry i is (i + r) mod 16 for one r of each draw.
All inputs are finite; a program needn't handle non-finite values.
Results may differ from a plain program's by a relative error of at most 0.015.
Values may be sent and summed in bfloat16 or wider, within the bound.
A program may use at most 64 MiB of HBM per device.

v0:
```python
import jax
import jax.numpy as jnp
from jax import lax
from jax.sharding import PartitionSpec as P

SF = 4
QROWS_DEV = 64


norm_epsilon = 1e-06
masked_score = -1e30


def extended(block, sides, width):
    for axis, dim in sides:
        count = lax.axis_size(axis)
        forward = [(i, i + 1) for i in range(count - 1)]
        forward.append((count - 1, 0))
        backward = [(target, source) for source, target in forward]
        low = lax.ppermute(
            lax.slice_in_dim(block, block.shape[dim] - width, None, axis=dim), axis, forward
        )
        high = lax.ppermute(lax.slice_in_dim(block, 0, width, axis=dim), axis, backward)
        block = jnp.concatenate([low, block, high], axis=dim)
    return block


def deliver_queries(placed, pair_count):
    slots = placed.reshape(pair_count, QROWS_DEV, placed.shape[1], placed.shape[2]).astype(
        jnp.bfloat16
    )
    received = lax.all_to_all(slots, "seq", split_axis=0, concat_axis=0, tiled=True)
    return jnp.sum(received.astype(jnp.float32), axis=0).astype(jnp.bfloat16)


def body(byte_rows, pool_weight, norm_gain, qkv_weight, span_order, query_start):
    local_rows, features = byte_rows.shape
    half_rows = local_rows // 2
    short_rows = local_rows // SF
    span_rows = short_rows // 2
    model_width = qkv_weight.shape[0]
    heads_here = qkv_weight.shape[1]
    head_width = qkv_weight.shape[3]
    pair_count = lax.axis_size("seq")
    seq_index = lax.axis_index("seq")
    head_index = lax.axis_index("head")
    pair_slots = jnp.arange(pair_count, dtype=jnp.int32)
    my_pair = jnp.sum(jnp.where(pair_slots == seq_index, span_order, 0))
    shift_rows = SF - 1
    first_tail = byte_rows[half_rows - shift_rows : half_rows]
    outgoing = jnp.concatenate([byte_rows[local_rows - shift_rows :], first_tail], axis=0)
    padded = extended(outgoing, (("seq", 0),), shift_rows)
    from_before = padded[:shift_rows]
    from_after = padded[padded.shape[0] - shift_rows :]
    first_prev = jnp.where(my_pair == 0, jnp.zeros_like(from_before), from_before)
    second_prev = jnp.where(my_pair == pair_count - 1, first_tail, from_after)
    grouped = jnp.concatenate(
        [
            first_prev,
            byte_rows[: half_rows - shift_rows],
            second_prev,
            byte_rows[half_rows : local_rows - shift_rows],
        ],
        axis=0,
    )
    grouped = grouped.reshape(short_rows, SF * features)
    partial_value = jnp.dot(
        grouped, pool_weight.reshape(SF * features, model_width), preferred_element_type=jnp.float32
    )
    qkv_flat = qkv_weight.reshape(model_width, heads_here * 3 * head_width)
    shortened = lax.psum_scatter(partial_value, "head", scatter_dimension=1, tiled=True).astype(
        jnp.bfloat16
    )
    widened = shortened.astype(jnp.float32)
    squares = lax.psum(jnp.sum(widened * widened, axis=1, keepdims=True), "head") / model_width
    gain_here = lax.dynamic_slice_in_dim(norm_gain, head_index * features, features, 0)
    normed_part = (widened * lax.rsqrt(squares + norm_epsilon) * gain_here).astype(jnp.bfloat16)
    projected = jnp.dot(
        lax.all_gather(normed_part, "head", axis=1, tiled=True),
        qkv_flat,
        preferred_element_type=jnp.float32,
    )
    projected = projected.astype(jnp.bfloat16).reshape(short_rows, heads_here, 3, head_width)
    own_spans = (my_pair, 2 * pair_count - 1 - my_pair)
    query_total = QROWS_DEV * pair_count
    window_start = query_start[0]
    own_queries = projected[:, :, 0]
    local_index = jnp.arange(span_rows, dtype=jnp.int32)

    def place_half(half_index):
        span_id = own_spans[half_index]
        positions = span_id * span_rows + local_index
        inside = (positions >= window_start) & (positions < window_start + query_total)
        rows_here = own_queries[half_index * span_rows : (half_index + 1) * span_rows].astype(
            jnp.float32
        )
        values_in = jnp.where(inside[:, None, None], rows_here, 0.0)
        at_row = jnp.clip(span_id * span_rows - window_start, -span_rows, query_total) + span_rows
        canvas = jnp.zeros((query_total + 2 * span_rows, heads_here, head_width), jnp.float32)
        return lax.dynamic_update_slice(canvas, values_in, (at_row, jnp.int32(0), jnp.int32(0)))

    placed = (place_half(0) + place_half(1))[span_rows : span_rows + query_total]
    my_queries = deliver_queries(placed, pair_count)
    score_scale = head_width ** (-0.5)

    def piece_positions(count):
        row_numbers = jnp.arange(count, dtype=jnp.int32)
        owner_dev = row_numbers // short_rows
        second = row_numbers // span_rows % 2
        owner_pair = jnp.sum(
            jnp.where(owner_dev[:, None] == pair_slots[None, :], span_order[None, :], 0), axis=1
        )
        span_id = jnp.where(second == 0, owner_pair, 2 * pair_count - 1 - owner_pair)
        return span_id * span_rows + row_numbers % span_rows

    def masked_scores(query_block, query_pos, key_block, key_pos):
        scores = (
            jnp.einsum("qhd,khd->hqk", query_block, key_block, preferred_element_type=jnp.float32)
            * score_scale
        )
        return jnp.where(key_pos[None, None, :] <= query_pos[None, :, None], scores, masked_score)

    query_pos = window_start + seq_index * QROWS_DEV + jnp.arange(QROWS_DEV, dtype=jnp.int32)
    portion = lax.all_gather(projected[:, :, 1], "seq", axis=0, tiled=True)
    scores = masked_scores(my_queries, query_pos, portion, piece_positions(portion.shape[0]))
    highest = jnp.maximum(
        jnp.full((heads_here, QROWS_DEV), masked_score, jnp.float32), jnp.max(scores, axis=2)
    )
    portion = lax.all_gather(projected[:, :, 1:], "seq", axis=0, tiled=True)
    scores = masked_scores(
        my_queries, query_pos, portion[:, :, 0], piece_positions(portion.shape[0])
    )
    weights = jnp.exp(scores - highest[:, :, None]).astype(jnp.bfloat16)
    summed = jnp.einsum(
        "hqk,khd->qhd", weights, portion[:, :, 1], preferred_element_type=jnp.float32
    )
    totals = jnp.sum(weights, axis=2, dtype=jnp.float32)
    summed, totals = (summed, totals)
    context = summed / totals.T[:, :, None]
    row_highest = highest * head_width**0.5
    return (
        shortened,
        context.reshape(QROWS_DEV, heads_here * head_width).astype(jnp.bfloat16),
        row_highest,
    )


def solution(mesh):
    placed = (P("seq", "head"), P(None, "head", None), P(), P(None, "head", None, None), P(), P())
    return jax.shard_map(
        body,
        mesh=mesh,
        in_specs=placed,
        out_specs=(P("seq", "head"), P("seq", "head"), P("head", "seq")),
        check_vma=False,
    )
```

profile of v0, /device:TPU:11, one launch (start us, length us, event | category | flops | bytes accessed | tf_op | source)
XLA Modules:
  0.0 213.9 jit_solution(7884034041708387243)
XLA Ops:
  7.2 0.7 slice.41
  7.9 0.7 collective-permute-start.1
  8.6 1.3 fusion.31
  10.5 1.3 collective-permute-done.1
  11.8 0.7 fusion.32
  12.6 0.7 collective-permute-start
  13.2 1.3 fusion.33
  15.4 1.5 reshape.135
  16.9 4.9 %fusion.34 = f32[256,1024]{1,0:T(8,128)} fusion(bf16[256,2048]{1,0:T(8,128)(2,1)} %reshape.135, bf16[2048,1024]{1,0:T(8,128)(2,1)} %bitcast.76), kind=kOutput, calls=%fused_computation.70 | convolution fusion | flops 1073741824 | bytes 6291456 | tf_op jit(solution)/shard_map/dot_general | solution.py:67
  21.9 4.4 %copy.33 = bf16[1024,4,3,128]{0,3,2,1:T(8,128)(2,1)} copy(bf16[1024,4,3,128]{3,1,2,0:T(4,128)(2,1)S(1)} %copy-done) | data formatting | bytes 6291456 | tf_op args[3]
  26.4 18.3 %reduce-scatter.2.cloned.1.call-done = f32[256,512]{1,0:T(8,128)} async-done(((f32[256,1024]{1,0:T(8,128)}), f32[256,512]{1,0:T(8,128)}) %reduce-scatter.2.cloned.1.call-update) | async-done | bytes 524304 | tf_op jit(solution)/shard_map/reduce_scatter | solution.py:71
  44.7 1.2 fusion.14
  45.9 3.8 %psum.7 = f32[256,1]{0,1:T(1,128)S(1)} all-reduce(f32[256,1]{0,1:T(1,128)S(1)} %bitcast.74), channel_id=1, replica_groups=mesh['seq'=16,'head'=2] {'head'}, use_global_device_ids=true, to_apply=%region_3.4 | all-reduce | flops 256 | bytes 2048 | tf_op jit(solution)/shard_map/psum | solution.py:75
  49.8 6.6 %all_gather.9 = bf16[256,1024]{1,0:T(8,128)(2,1)S(1)} all-gather(bf16[256,512]{1,0:T(8,128)(2,1)S(1)} %fusion.16), channel_id=1, replica_groups=mesh['seq'=16,'head'=2] {'head'}, dimensions={1}, use_global_device_ids=true | all-gather | bytes 786432 | tf_op jit(solution)/shard_map/all_gather | solution.py:79
  56.5 2.9 %convolution_convert_fusion = bf16[256,1536]{1,0:T(8,128)(2,1)S(1)} fusion(bf16[256,1024]{1,0:T(8,128)(2,1)S(1)} %all_gather.9, bf16[1024,1536]{0,1:T(8,128)(2,1)} %bitcast.72), kind=kOutput, calls=%fused_computation.12 | convolution fusion | flops 805699584 | bytes 4456448 | tf_op jit(solution)/shard_map/dot_general | solution.py:78
  59.7 0.8 copy.43
  60.6 1.0 copy.42
  63.6 0.7 convert_select_fusion.1
  64.6 1.4 dynamic_update_slice.8
  66.0 0.9 fusion.17
  66.9 2.2 %add.128 = f32[1280,4,128]{0,2,1:T(8,128)S(1)} dynamic-update-slice(f32[1280,4,128]{0,2,1:T(8,128)S(1)} %dynamic_update_slice.8, f32[128,4,128]{0,2,1:T(8,128)} %fusion.17, s32[]{:T(128)S(6)} %select_n.109, s32[]{:T(128)} %constant.88.clone.1, s32[]{:T(128)} %constant.88.clone.1) | dynamic-update-slice | bytes 524292 | tf_op jit(solution)/shard_map/add | solution.py:102
  69.1 1.2 slice.77
  70.3 1.6 copy.37
  71.9 1.1 copy.38
  73.1 7.5 %all-to-all-start = ((bf16[16,64,4,128]{3,1,2,0:T(8,128)(2,1)}), bf16[16,64,4,128]{3,1,2,0:T(8,128)(2,1)S(1)}, u32[]{:S(2)}, u32[]{:S(2)}) async-start(bf16[16,64,4,128]{3,1,2,0:T(8,128)(2,1)} %copy.38), calls=%async_computation.1 | async-start | bytes 2097152 | tf_op jit(solution)/shard_map/all_to_all | solution.py:32
  81.0 41.0 %all-to-all-done = bf16[16,64,4,128]{3,1,2,0:T(8,128)(2,1)S(1)} async-done(((bf16[16,64,4,128]{3,1,2,0:T(8,128)(2,1)}), bf16[16,64,4,128]{3,1,2,0:T(8,128)(2,1)S(1)}, u32[]{:S(2)}, u32[]{:S(2)}) %all-to-all-start) | async-done | bytes 1048608 | tf_op jit(solution)/shard_map/all_to_all | solution.py:32
  122.2 1.4 all-gather.6.cloned.1.call-done
  123.5 3.8 %fusion.7 = f32[4,64]{1,0:T(4,128)S(1)} fusion(bf16[64,4,128]{2,0,1:T(8,128)(2,1)S(1)} %reduce_sum.55, bf16[4096,4,1,128]{3,0,1,2:T(8,128)(2,1)} %all-gather.6.cloned.1.call-done, pred[64,4096]{1,0:T(8,128)(4,1)S(1)} %broadcast_compare_fusion), kind=kOutput, calls=%fused_computation.14 | convolution fusion | flops 271580928 | bytes 4523008 | tf_op jit(solution)/shard_map/qhd,khd->hqk/dot_general | solution.py:118
  128.0 73.2 %all-gather.4.cloned.1.call-done = bf16[4096,4,2,128]{3,0,1,2:T(8,128)(2,1)} async-done(((bf16[256,4,2,128]{3,0,1,2:T(8,128)(2,1)}), bf16[4096,4,2,128]{3,0,1,2:T(8,128)(2,1)}) %all-gather.4.cloned.1.call-update) | async-done | bytes 8388624 | tf_op jit(solution)/shard_map/all_gather | solution.py:129
  201.2 4.1 %convert_reduce_fusion = (f32[4,64]{1,0:T(4,128)S(1)}, bf16[4,64,4096]{2,1,0:T(8,128)(2,1)S(1)}) fusion(f32[4,64]{1,0:T(4,128)S(1)} %get-tuple-element.10, bf16[64,4,128]{2,0,1:T(8,128)(2,1)S(1)} %reduce_sum.55, bf16[4096,4,2,128]{3,0,1,2:T(8,128)(2,1)} %all-gather.4.cloned.1.call-done, pred[64,4096]{1,0:T(8,128)(4,1)S(1)} %broadcast_compare_fusion), kind=kOutput, calls=%fused_computation.11 | convolution fusion | flops 274726656 | bytes 6621184 | tf_op jit(solution)/shard_map/qhd,khd->hqk/dot_general | solution.py:118
  205.8 0.8 fusion.13
  206.7 0.6 copy.46
  (35 shorter events, 2.9 us)
Async XLA Ops:
  7.2 37.5 %reduce-scatter.2.cloned.1.call-start = ((), (), s32[]{:S(2)}) async-start(), calls=%async_computation.2 | async-start | bytes 1572864 | tf_op jit(solution)/shard_map/reduce_scatter | solution.py:71
  7.9 3.9 %collective-permute-start.1 = (bf16[3,512]{1,0:T(4,128)(2,1)S(1)}, bf16[3,512]{1,0:T(4,128)(2,1)S(1)}, u32[]{:S(2)}, u32[]{:S(2)}) collective-permute-start(bf16[3,512]{1,0:T(4,128)(2,1)S(1)} %slice.41), channel_id=1, source_target_pairs={{2,0},{4,2},{6,4},{8,6},{10,8},{12,10},{14,12},{16,14},{18,16},{20... | collective-permute-start | bytes 9224 | tf_op jit(solution)/shard_map/ppermute | solution.py:23
  12.6 2.6 %collective-permute-start = (bf16[3,512]{1,0:T(4,128)(2,1)S(1)}, bf16[3,512]{1,0:T(4,128)(2,1)S(1)}, u32[]{:S(2)}, u32[]{:S(2)}) collective-permute-start(bf16[3,512]{1,0:T(4,128)(2,1)S(1)} %get-tuple-element.5), channel_id=1, source_target_pairs={{0,2},{2,4},{4,6},{6,8},{8,10},{10,12},{12,14},{14,16},{16,18},{18... | collective-permute-start | bytes 9224 | tf_op jit(solution)/shard_map/ppermute | solution.py:20
  16.9 5.0 %copy-start = (bf16[1024,4,3,128]{3,1,2,0:T(4,128)(2,1)S(1)}, bf16[1024,4,3,128]{3,1,2,0:T(4,128)(2,1)}, u32[]{:S(2)}) copy-start(bf16[1024,4,3,128]{3,1,2,0:T(4,128)(2,1)} %param.9) | copy-start | bytes 9437188
  21.8 4.5 %copy-start.2 = (f32[1024]{0:T(1024)S(1)}, f32[1024]{0:T(1024)}, u32[]{:S(2)}) copy-start(f32[1024]{0:T(1024)} %param.8) | copy-start | bytes 12292
  21.8 101.7 %all-gather.6.cloned.1.call-start = ((), (), s32[]{:S(2)}) async-start(), calls=%async_computation.4 | async-start | bytes 4456448 | tf_op jit(solution)/shard_map/all_gather | solution.py:124
  45.9 10.6 %copy-start.1 = (bf16[256,512]{1,0:T(8,128)(2,1)}, bf16[256,512]{1,0:T(8,128)(2,1)S(1)}, u32[]{:S(2)}) copy-start(bf16[256,512]{1,0:T(8,128)(2,1)S(1)} %get-tuple-element.4) | copy-start | bytes 786436
  60.5 140.7 %all-gather.4.cloned.1.call-start = ((), (), s32[]{:S(2)}) async-start(), calls=%async_computation.3 | async-start | bytes 8912896 | tf_op jit(solution)/shard_map/all_gather | solution.py:129
  69.1 11.6 %copy-start.3 = (s32[16]{0:T(128)S(1)}, s32[16]{0:T(128)}, u32[]{:S(2)}) copy-start(s32[16]{0:T(128)} %param.10) | copy-start | bytes 196
  73.1 48.9 %all-to-all-start = ((bf16[16,64,4,128]{3,1,2,0:T(8,128)(2,1)}), bf16[16,64,4,128]{3,1,2,0:T(8,128)(2,1)S(1)}, u32[]{:S(2)}, u32[]{:S(2)}) async-start(bf16[16,64,4,128]{3,1,2,0:T(8,128)(2,1)} %copy.38), calls=%async_computation.1 | async-start | bytes 2097152 | tf_op jit(solution)/shard_map/all_to_all | solution.py:32
  201.2 4.6 %copy-start.4 = (bf16[4096,4,2,128]{3,0,1,2:T(8,128)(2,1)S(1)}, bf16[4096,4,2,128]{3,0,1,2:T(8,128)(2,1)}, u32[]{:S(2)}) copy-start(bf16[4096,4,2,128]{3,0,1,2:T(8,128)(2,1)} %all-gather.4.cloned.1.call-done) | copy-start | bytes 25165828
Sparse Core Ops, SparseCore 0:
  21.9 22.7 reduce-scatter.1
  60.7 62.8 all-gather.5
  126.0 75.1 all-gather.3
where the time goes:
time: 217 us; the launch traced here: 214 us
  waiting for transfers between devices  135 us (62%)
  local copies, waits for them, and re-layouts  19.1 us (9%)
  between operations  17.2 us (8%)
  matrix products  16.6 us (8%)
  blocking collectives  10.4 us (5%)
  starting transfers between devices  8.99 us (4%)
  other arithmetic  6.3 us (3%)
    all_gather x1, waiting for transfers between devices, body(): portion = lax.all_gather(projected[:, :, 1:], 'seq', axis=0, tiled=True)  73.2 us
    all_to_all x1, waiting for transfers between devices, deliver_queries(): lax.all_to_all(slots, 'seq', split_axis=0, concat_axis=0, tiled=True)  41 us
    reduce_scatter x1, waiting for transfers between devices, body(): lax.psum_scatter(partial_value, 'head', scatter_dimension=1, tiled=True)  18.3 us
    dot_general x2, matrix products, masked_scores(): jnp.einsum('qhd,khd->hqk', query_block, key_block, preferred_element_type...  7.97 us
    all_to_all x1, starting transfers between devices, deliver_queries(): lax.all_to_all(slots, 'seq', split_axis=0, concat_axis=0, tiled=True)  7.52 us
    unnamed x13, local copies, waits for them, and re-layouts  6.76 us
    all_gather x1, blocking collectives, body(): lax.all_gather(normed_part, 'head', axis=1, tiled=True)  6.65 us
    dot_general x1, matrix products, body(): jnp.dot(grouped, pool_weight.reshape(SF * features, model_width), preferr...  4.88 us
  transfers between devices with their start and end apart: 6, of which 5 were waited for; matrix products, arithmetic and copies ran while one was open for 11% of the time, Pallas kernels for 0%

commit v1 on v0

v1 whole, which is shorter than its diff:
```python
import jax
import jax.numpy as jnp
from jax import lax
from jax.sharding import PartitionSpec as P

SF = 4
QROWS_DEV = 64


norm_epsilon = 1e-06
masked_score = -1e30


def ring(count, step):
    return [(i, (i + step) % count) for i in range(count)]


def body(byte_rows, pool_weight, norm_gain, qkv_weight, span_order, query_start):
    local_rows, features = byte_rows.shape
    half_rows = local_rows // 2
    short_rows = local_rows // SF
    span_rows = short_rows // 2
    model_width = qkv_weight.shape[0]
    heads_here = qkv_weight.shape[1]
    head_width = qkv_weight.shape[3]
    width_here = heads_here * head_width
    pair_count = lax.axis_size("seq")
    head_count = lax.axis_size("head")
    seq_index = lax.axis_index("seq")
    head_index = lax.axis_index("head")
    pair_slots = jnp.arange(pair_count, dtype=jnp.int32)
    my_pair = jnp.sum(jnp.where(pair_slots == seq_index, span_order, 0))
    shift_rows = SF - 1
    first_tail = byte_rows[half_rows - shift_rows : half_rows]
    last_tail = byte_rows[local_rows - shift_rows :]
    from_before = lax.ppermute(first_tail, "seq", ring(pair_count, 1))
    from_after = lax.ppermute(last_tail, "seq", ring(pair_count, -1))
    first_prev = jnp.where(my_pair == 0, jnp.zeros_like(from_before), from_before)
    second_prev = jnp.where(my_pair == pair_count - 1, first_tail, from_after)
    grouped = jnp.concatenate(
        [
            first_prev,
            byte_rows[: half_rows - shift_rows],
            second_prev,
            byte_rows[half_rows : local_rows - shift_rows],
        ],
        axis=0,
    )
    grouped = grouped.reshape(short_rows, SF * features)
    partial = jnp.dot(
        grouped, pool_weight.reshape(SF * features, model_width), preferred_element_type=jnp.float32
    )
    sent = partial.astype(jnp.bfloat16)
    total = partial
    for step in range(1, head_count):
        total = total + lax.ppermute(sent, "head", ring(head_count, step)).astype(jnp.float32)
    pooled = total.astype(jnp.bfloat16)
    shortened = lax.dynamic_slice_in_dim(pooled, head_index * features, features, 1)
    widened = pooled.astype(jnp.float32)
    squares = jnp.sum(widened * widened, axis=1, keepdims=True) / model_width
    normed = (widened * lax.rsqrt(squares + norm_epsilon) * norm_gain).astype(jnp.bfloat16)
    projected = jnp.einsum(
        "rm,mhtd->thrd", normed, qkv_weight, preferred_element_type=jnp.float32
    ).astype(jnp.bfloat16)
    keys, values = projected[1], projected[2]
    half_short = pair_count * span_rows
    query_total = QROWS_DEV * pair_count
    window_start = query_start[0]
    late = lax.all_gather(projected[0][:, span_rows:], "seq", axis=0, tiled=False)
    late = jnp.concatenate([late[::-1], late[::-1]], axis=0)
    late = late.transpose(1, 0, 2, 3).reshape(heads_here, 2 * half_short, head_width)
    at_row = span_order[0] * span_rows + window_start - half_short
    queries = lax.dynamic_slice_in_dim(late, at_row, query_total, 1)
    score_scale = head_width ** (-0.5)
    local = jnp.arange(short_rows, dtype=jnp.int32)
    span_id = jnp.where(local < span_rows, my_pair, 2 * pair_count - 1 - my_pair)
    key_pos = span_id * span_rows + local % span_rows
    query_pos = window_start + jnp.arange(query_total, dtype=jnp.int32)
    scores = (
        jnp.einsum("hqd,hkd->hqk", queries, keys, preferred_element_type=jnp.float32) * score_scale
    )
    scores = jnp.where(key_pos[None, None, :] <= query_pos[None, :, None], scores, masked_score)
    highest = jnp.max(scores, axis=2)
    weights = jnp.exp(scores - highest[:, :, None]).astype(jnp.bfloat16)
    totals = jnp.sum(weights, axis=2, dtype=jnp.float32)
    summed = jnp.einsum("hqk,hkd->qhd", weights, values, preferred_element_type=jnp.float32)
    summed = summed.astype(jnp.bfloat16).reshape(query_total, width_here)
    stats = jnp.stack([highest, totals], axis=0).reshape(2, heads_here, pair_count, QROWS_DEV)
    stats = stats.transpose(2, 0, 1, 3)
    summed = lax.all_to_all(summed, "seq", split_axis=0, concat_axis=0, tiled=True)
    stats = lax.all_to_all(stats, "seq", split_axis=0, concat_axis=0, tiled=True)
    summed = summed.reshape(pair_count, QROWS_DEV, heads_here, head_width).astype(jnp.float32)
    highs, tots = stats[:, 0], stats[:, 1]
    top = jnp.max(highs, axis=0)
    factor = jnp.exp(highs - top[None])
    denominator = jnp.sum(factor * tots, axis=0)
    numerator = jnp.sum(summed * factor.transpose(0, 2, 1)[..., None], axis=0)
    context = numerator / denominator.T[:, :, None]
    row_highest = top * head_width**0.5
    return (
        shortened,
        context.reshape(QROWS_DEV, width_here).astype(jnp.bfloat16),
        row_highest,
    )


def solution(mesh):
    placed = (P("seq", "head"), P(None, "head", None), P(), P(None, "head", None, None), P(), P())
    return jax.shard_map(
        body,
        mesh=mesh,
        in_specs=placed,
        out_specs=(P("seq", "head"), P("seq", "head"), P("head", "seq")),
        check_vma=False,
    )
```

time: 217 us -> 159 us (0.73); the launches traced: 214 us -> 158 us
  waiting for transfers between devices: 135 us -> 68.5 us
  local copies, waits for them, and re-layouts: 19.1 us -> 29.8 us
  blocking collectives: 10.4 us -> 0 us
  other arithmetic: 6.3 us -> 15.5 us
  starting transfers between devices: 8.99 us -> 14.4 us
  matrix products: 16.6 us -> 13.4 us
    all_gather x2 -> x1, waiting for transfers between devices: 74.6 us -> 40.8 us  [body(): lax.all_gather(projected[0][:, span_rows:], 'seq', axis=0, tiled=False)]
    all_to_all x1 -> x2, waiting for transfers between devices: 41 us -> 13.9 us  [the longest x1 13.9 us: body(): lax.all_to_all(summed, 'seq', split_axis=0, concat_axis=0, tiled=True)]
    reduce_scatter x1 -> x0, waiting for transfers between devices: 18.3 us -> none  [body(): lax.psum_scatter(partial_value, 'head', scatter_dimension=1, tiled=True)]
    ppermute x2 -> x3, waiting for transfers between devices: 1.31 us -> 13.7 us  [the longest x1 12.4 us: body(): lax.ppermute(sent, 'head', ring(head_count, step)).astype(jnp.float32)]
    all_gather x1 -> x0, blocking collectives: 6.65 us -> none  [body(): lax.all_gather(normed_part, 'head', axis=1, tiled=True)]
    mul x0 -> x2, local copies, waits for them, and re-layouts: none -> 6.27 us  [body(): numerator = jnp.sum(summed * factor.transpose(0, 2, 1)[..., None], axis=0)]
    unnamed x13 -> x12, local copies, waits for them, and re-layouts: 6.76 us -> 2.52 us
    all_to_all x1 -> x2, starting transfers between devices: 7.52 us -> 11.7 us  [the longest x1 6.02 us: body(): lax.all_to_all(summed, 'seq', split_axis=0, concat_axis=0, tiled=True)]
  transfers between devices with their start and end apart: 6 -> 6, of which waited for: 5 -> 4; matrix products, arithmetic and copies ran while one was open for 11% -> 14% of each run, Pallas kernels for 0% -> 0%
where the time goes in v1:
time: 159 us; the launch traced here: 158 us
  waiting for transfers between devices  68.5 us (43%)
  local copies, waits for them, and re-layouts  29.8 us (19%)
  between operations  16.8 us (11%)
  other arithmetic  15.5 us (10%)
  starting transfers between devices  14.4 us (9%)
  matrix products  13.4 us (8%)
    all_gather x1, waiting for transfers between devices, body(): lax.all_gather(projected[0][:, span_rows:], 'seq', axis=0, tiled=False)  40.8 us
    all_to_all x1, waiting for transfers between devices, body(): lax.all_to_all(summed, 'seq', split_axis=0, concat_axis=0, tiled=True)  13.9 us
    ppermute x1, waiting for transfers between devices, body(): lax.ppermute(sent, 'head', ring(head_count, step)).astype(jnp.float32)  12.4 us
    mul x2, local copies, waits for them, and re-layouts, body(): numerator = jnp.sum(summed * factor.transpose(0, 2, 1)[..., None], axis=0)  6.27 us
    all_to_all x1, starting transfers between devices, body(): lax.all_to_all(summed, 'seq', split_axis=0, concat_axis=0, tiled=True)  6.02 us
    all_to_all x1, starting transfers between devices, body(): lax.all_to_all(stats, 'seq', split_axis=0, concat_axis=0, tiled=True)  5.71 us
    dot_general x1, matrix products, body(): jnp.einsum('hqk,hkd->qhd', weights, values, preferred_element_type=jnp.fl...  4.53 us
    dot_general x1, matrix products, body(): jnp.einsum('hqd,hkd->hqk', queries, keys, preferred_element_type=jnp.floa...  4.06 us
  transfers between devices with their start and end apart: 6, of which 4 were waited for; matrix products, arithmetic and copies ran while one was open for 14% of the time, Pallas kernels for 0%

profile of v1, /device:TPU:11, one launch (start us, length us, event | category | flops | bytes accessed | tf_op | source)
XLA Modules:
  0.0 158.4 jit_solution(8788710524341108350)
XLA Ops:
  7.2 0.9 slice.35
  8.8 1.3 fusion.26
  10.7 1.3 collective-permute-done.1
  12.0 0.7 fusion.28
  13.4 2.3 %fusion.29 = (bf16[509,512]{1,0:T(8,128)(2,1)}, bf16[509,512]{1,0:T(8,128)(2,1)}) fusion(bf16[1024,512]{1,0:T(8,128)(2,1)} %param.6), kind=kLoop, calls=%fused_computation.52 | loop fusion | bytes 2084864 | tf_op jit(solution)/shard_map/slice | solution.py:43
  16.4 2.4 %pad_maximum_fusion.1 = bf16[1024,512]{1,0:T(8,128)(2,1)} fusion(bf16[509,512]{1,0:T(8,128)(2,1)} %get-tuple-element.8, bf16[3,512]{1,0:T(4,128)(2,1)S(1)} %get-tuple-element.6, bf16[509,512]{1,0:T(8,128)(2,1)} %get-tuple-element.7, bf16[3,512]{1,0:T(4,128)(2,1)S(1)} %broadcast_select_fusion.1), kind=kLoop, calls=%fused_computation.17 | loop fusion | flops 4194304 | bytes 2097152 | tf_op jit(solution)/shard_map/concatenate | solution.py:40
  18.8 2.5 %reshape.97 = bf16[256,2048]{1,0:T(8,128)(2,1)} reshape(bf16[1024,512]{1,0:T(8,128)(2,1)} %pad_maximum_fusion.1) | data formatting | bytes 2097152 | tf_op jit(solution)/shard_map/reshape | solution.py:49
  21.3 3.8 %fusion.30 = (bf16[256,1024]{1,0:T(8,128)(2,1)S(1)}, f32[256,1024]{1,0:T(8,128)S(1)}) fusion(bf16[256,2048]{1,0:T(8,128)(2,1)} %reshape.97, bf16[2048,1024]{1,0:T(8,128)(2,1)} %bitcast.62), kind=kOutput, calls=%fused_computation.53 | convolution fusion | flops 1074003968 | bytes 6815744 | tf_op jit(solution)/shard_map/dot_general | solution.py:50
  25.1 1.3 collective-permute-start.2
  26.4 12.4 %collective-permute-done.2 = bf16[256,1024]{1,0:T(8,128)(2,1)S(1)} collective-permute-done((bf16[256,1024]{1,0:T(8,128)(2,1)S(1)}, bf16[256,1024]{1,0:T(8,128)(2,1)S(1)}, u32[]{:S(2)}, u32[]{:S(2)}) %collective-permute-start.2) | collective-permute-done | bytes 524320 | tf_op jit(solution)/shard_map/ppermute | solution.py:56
  39.1 0.8 copy-done.1
  39.8 1.1 fusion.7
  40.9 0.9 copy-done.2
  44.8 40.8 %all-gather.3.cloned.1.call-done = bf16[64,128,128]{2,1,0:T(8,128)(2,1)} async-done(((bf16[4,128,128]{2,1,0:T(8,128)(2,1)}), bf16[64,128,128]{2,1,0:T(8,128)(2,1)}) %all-gather.3.cloned.1.call-update) | async-done | bytes 2097168 | tf_op jit(solution)/shard_map/all_gather | solution.py:69
  85.6 3.1 %copy.29 = bf16[16,4,128,128]{3,2,0,1:T(8,128)(2,1)} copy(bf16[16,4,128,128]{3,2,1,0:T(8,128)(2,1)} %bitcast.59) | data formatting | bytes 4194304 | tf_op jit(solution)/shard_map/all_gather | solution.py:69
  88.8 3.2 %rev.4 = bf16[16,4,128,128]{3,2,0,1:T(8,128)(2,1)} reverse(bf16[16,4,128,128]{3,2,0,1:T(8,128)(2,1)} %copy.29), dimensions={0} | reverse | bytes 4194304 | tf_op jit(solution)/shard_map/rev | solution.py:70
  91.9 2.6 %pad_maximum_fusion = bf16[32,4,128,128]{3,2,0,1:T(8,128)(2,1)S(1)} fusion(bf16[16,4,128,128]{3,2,0,1:T(8,128)(2,1)} %rev.4), kind=kLoop, calls=%fused_computation | loop fusion | flops 2097152 | bytes 6291456 | tf_op jit(solution)/shard_map/concatenate | solution.py:70
  94.5 4.1 %fusion = (f32[4,1024]{1,0:T(4,128)S(1)}, f32[4,1024,256]{1,2,0:T(8,128)}) fusion(pred[1024,256]{0,1:T(8,128)(4,1)S(1)} %broadcast_compare_fusion, bf16[3,4,256,128]{3,2,0,1:T(8,128)(2,1)} %copy-done.2, bf16[4,4096,128]{2,1,0:T(8,128)(2,1)S(1)} %bitcast.58, s32[]{:T(128)S(6)} %select_n.55), kind=kOutput, calls=%fused_computation.4 | convolution fusion | flops 271577088 | bytes 5783556 | tf_op jit(solution)/shard_map/hqd,hkd->hqk/dot_general | solution.py:80
  98.7 3.1 %convert_reduce_fusion = f32[4,1024]{1,0:T(4,128)S(1)} fusion(f32[4,1024]{1,0:T(4,128)S(1)} %get-tuple-element.13, f32[4,1024,256]{1,2,0:T(8,128)} %get-tuple-element.14, pred[1024,256]{0,1:T(8,128)(4,1)S(1)} %broadcast_compare_fusion), kind=kLoop, calls=%fused_computation.1 | loop fusion | flops 6287360 | bytes 4489216 | tf_op jit(solution)/shard_map/reduce_sum | solution.py:85
  101.9 0.7 reshape.102
  102.6 5.7 %all-to-all-start.1 = ((f32[16,1,512]{2,1,0:T(1,128)}), f32[16,1,512]{2,1,0:T(1,128)S(1)}, u32[]{:S(2)}, u32[]{:S(2)}) async-start(f32[16,1,512]{2,1,0:T(1,128)} %reshape.102), calls=%async_computation.1 | async-start | bytes 65536 | tf_op jit(solution)/shard_map/all_to_all | solution.py:91
  108.3 4.5 %fusion.6 = bf16[1024,4,128]{0,2,1:T(8,128)(2,1)} fusion(bf16[3,4,256,128]{3,2,0,1:T(8,128)(2,1)} %copy-done.2, f32[4,1024,256]{1,2,0:T(8,128)} %get-tuple-element.14, f32[4,1024]{1,0:T(4,128)S(1)} %get-tuple-element.13, pred[1024,256]{0,1:T(8,128)(4,1)S(1)} %broadcast_compare_fusion), kind=kOutput, calls=%fused_computation.10 | convolution fusion | flops 273154048 | bytes 5783552 | tf_op jit(solution)/shard_map/hqk,hkd->qhd/dot_general | solution.py:86
  112.9 2.4 %copy.32 = bf16[1024,4,128]{2,1,0:T(4,128)(2,1)} copy(bf16[1024,4,128]{0,2,1:T(8,128)(2,1)} %fusion.6) | data formatting | bytes 2097152 | tf_op jit(solution)/shard_map/convert_element_type | solution.py:87
  115.3 2.3 %all_to_all.9 = bf16[16,64,512]{2,1,0:T(8,128)(2,1)} reshape(bf16[1024,4,128]{2,1,0:T(4,128)(2,1)} %copy.32) | data formatting | bytes 2097152 | tf_op jit(solution)/shard_map/all_to_all | solution.py:90
  117.6 6.0 %all-to-all-start = ((bf16[16,64,512]{2,1,0:T(8,128)(2,1)}), bf16[16,64,512]{2,1,0:T(8,128)(2,1)}, u32[]{:S(2)}, u32[]{:S(2)}) async-start(bf16[16,64,512]{2,1,0:T(8,128)(2,1)} %all_to_all.9), calls=%async_computation | async-start | bytes 2097152 | tf_op jit(solution)/shard_map/all_to_all | solution.py:90
  123.6 1.7 %constant_dynamic-slice_fusion = bf16[256,512]{1,0:T(8,128)(2,1)} fusion(bf16[256,1024]{1,0:T(8,128)(2,1)} %copy-done.1, s32[]{:T(128)S(6)} %select_n.52), kind=kLoop, calls=%fused_computation.50 | loop fusion | bytes 524292 | tf_op jit(solution)/shard_map/dynamic_slice | solution.py:58
  125.8 0.7 reduce.2
  126.7 1.0 copy.35
  127.8 3.2 %mul.72 = f32[16,64,4,128]{3,2,1,0:T(4,128)} broadcast(f32[16,64,4]{2,1,0:T(8,128)} %copy.35), dimensions={0,1,2} | broadcast | bytes 2113536 | tf_op jit(solution)/shard_map/mul | solution.py:97
  130.9 3.1 %mul.73 = f32[16,64,512]{2,1,0:T(8,128)} reshape(f32[16,64,4,128]{3,2,1,0:T(4,128)} %mul.72) | data formatting | bytes 4194304 | tf_op jit(solution)/shard_map/mul | solution.py:97
  134.6 13.9 %all-to-all-done = bf16[16,64,512]{2,1,0:T(8,128)(2,1)} async-done(((bf16[16,64,512]{2,1,0:T(8,128)(2,1)}), bf16[16,64,512]{2,1,0:T(8,128)(2,1)}, u32[]{:S(2)}, u32[]{:S(2)}) %all-to-all-start) | async-done | bytes 1048608 | tf_op jit(solution)/shard_map/all_to_all | solution.py:90
  148.6 2.2 %multiply_reduce_fusion = f32[64,512]{1,0:T(8,128)S(1)} fusion(f32[16,64,512]{2,1,0:T(8,128)} %mul.73, bf16[16,64,512]{2,1,0:T(8,128)(2,1)} %all-to-all-done), kind=kLoop, calls=%fused_computation.7 | loop fusion | flops 1540096 | bytes 3276800 | tf_op jit(solution)/shard_map/reduce_sum | solution.py:97
  (34 shorter events, 5.6 us)
Async XLA Ops:
  7.2 32.7 %copy-start = (bf16[1024,4,3,128]{3,1,2,0:T(4,128)(2,1)S(1)}, bf16[1024,4,3,128]{3,1,2,0:T(4,128)(2,1)}, u32[]{:S(2)}) copy-start(bf16[1024,4,3,128]{3,1,2,0:T(4,128)(2,1)} %param.9) | copy-start | bytes 9437188
  7.2 78.4 %all-gather.3.cloned.1.call-start = ((), (), s32[]{:S(2)}) async-start(), calls=%async_computation.2 | async-start | bytes 2228224 | tf_op jit(solution)/shard_map/all_gather | solution.py:69
  8.1 3.9 %collective-permute-start.1 = (bf16[3,512]{1,0:T(4,128)(2,1)S(1)}, bf16[3,512]{1,0:T(4,128)(2,1)S(1)}, u32[]{:S(2)}, u32[]{:S(2)}) collective-permute-start(bf16[3,512]{1,0:T(4,128)(2,1)S(1)} %slice.35), channel_id=1, source_target_pairs={{0,30},{2,0},{4,2},{6,4},{8,6},{10,8},{12,10},{14,12},{16,14},{18,... | collective-permute-start | bytes 9224 | tf_op jit(solution)/shard_map/ppermute | solution.py:37
  12.7 3.6 %collective-permute-start = (bf16[3,512]{1,0:T(4,128)(2,1)S(1)}, bf16[3,512]{1,0:T(4,128)(2,1)S(1)}, u32[]{:S(2)}, u32[]{:S(2)}) collective-permute-start(bf16[3,512]{1,0:T(4,128)(2,1)S(1)} %get-tuple-element.5), channel_id=1, source_target_pairs={{0,2},{2,4},{4,6},{6,8},{8,10},{10,12},{12,14},{14,16},{16,18},{18... | collective-permute-start | bytes 9224 | tf_op jit(solution)/shard_map/ppermute | solution.py:36
  21.3 18.5 %copy-start.3 = (f32[1024]{0:T(1024)S(1)}, f32[1024]{0:T(1024)}, u32[]{:S(2)}) copy-start(f32[1024]{0:T(1024)} %param.8) | copy-start | bytes 12292
  25.1 13.7 %collective-permute-start.2 = (bf16[256,1024]{1,0:T(8,128)(2,1)S(1)}, bf16[256,1024]{1,0:T(8,128)(2,1)S(1)}, u32[]{:S(2)}, u32[]{:S(2)}) collective-permute-start(bf16[256,1024]{1,0:T(8,128)(2,1)S(1)} %get-tuple-element.11), channel_id=1, source_target_pairs={{0,1},{1,0},{2,3},{3,2},{4,5},{5,4},{6,7},{7,6},{8,9},{9,8},{10,11... | collective-permute-start | bytes 1572872 | tf_op jit(solution)/shard_map/ppermute | solution.py:56
  39.0 0.8 copy-start.1
  39.0 4.2 %copy-start.4 = (s32[16]{0:T(128)S(1)}, s32[16]{0:T(128)}, u32[]{:S(2)}) copy-start(s32[16]{0:T(128)} %param.10) | copy-start | bytes 196
  40.9 0.9 copy-start.2
  102.6 14.9 %all-to-all-start.1 = ((f32[16,1,512]{2,1,0:T(1,128)}), f32[16,1,512]{2,1,0:T(1,128)S(1)}, u32[]{:S(2)}, u32[]{:S(2)}) async-start(f32[16,1,512]{2,1,0:T(1,128)} %reshape.102), calls=%async_computation.1 | async-start | bytes 65536 | tf_op jit(solution)/shard_map/all_to_all | solution.py:91
  117.6 31.0 %all-to-all-start = ((bf16[16,64,512]{2,1,0:T(8,128)(2,1)}), bf16[16,64,512]{2,1,0:T(8,128)(2,1)}, u32[]{:S(2)}, u32[]{:S(2)}) async-start(bf16[16,64,512]{2,1,0:T(8,128)(2,1)} %all_to_all.9), calls=%async_computation | async-start | bytes 2097152 | tf_op jit(solution)/shard_map/all_to_all | solution.py:90
Sparse Core Ops, SparseCore 0:
  42.7 42.9 all-gather.2

commit v2 on v1

v2 whole, which is shorter than its diff:
```python
import functools

import jax
import jax.numpy as jnp
from jax import lax
from jax.experimental import pallas as pl
from jax.experimental.pallas import tpu as pltpu
from jax.sharding import PartitionSpec as P

SF = 4
QROWS_DEV = 64


norm_epsilon = 1e-06
masked_score = -1e30


def ring(count, step):
    return [(i, (i + step) % count) for i in range(count)]


LANES = 128
STAT_STEP = 16


def pack_stats(highest, totals):
    high_top = highest.astype(jnp.bfloat16).astype(jnp.float32)
    rest = highest - high_top
    high_mid = rest.astype(jnp.bfloat16).astype(jnp.float32)
    high_low = rest - high_mid
    total_top = totals.astype(jnp.bfloat16).astype(jnp.float32)
    total_low = totals - total_top
    packed = high_top
    for place, piece in enumerate((high_mid, high_low, total_top, total_low)):
        packed = packed + pltpu.roll(piece, STAT_STEP * (place + 1), 1)
    return packed


def unpack_stats(packed):
    def piece(place):
        return pltpu.roll(packed, LANES - STAT_STEP * place, 1)

    return packed + piece(1) + piece(2), piece(3) + piece(4)


def attend_kernel(
    count, heads, width, numbers, projected, context, top_out,
    gathered, parts, arrived, gather_send, gather_recv, part_send, part_recv,
):
    me = lax.axis_index("seq")
    core = lax.rem(me, 2)
    middle = lax.rem(me // 2, 2)
    outer = me // 4
    outers = count // 4
    rows = projected.shape[0]
    span = rows // 2
    total_width = heads * width

    def at(outer_at, middle_at, core_at):
        return (lax.rem(outer_at, outers) * 2 + middle_at) * 2 + core_at

    barrier = pltpu.get_barrier_semaphore()

    def greet(step, carry):
        pl.semaphore_signal(
            barrier, inc=1, device_id={"seq": lax.rem(me + step, count)},
            device_id_type=pl.DeviceIdType.MESH,
        )
        return carry

    lax.fori_loop(1, count, greet, 0)
    for head in range(heads):
        gathered[me, :, head * width : (head + 1) * width] = projected[
            span:, head * 3 * width : (head * 3 + 1) * width
        ]
    pl.semaphore_wait(barrier, count - 1)

    pushes = []

    def push(slot, target):
        copy = pltpu.make_async_remote_copy(
            src_ref=gathered.at[slot], dst_ref=gathered.at[slot],
            send_sem=gather_send.at[len(pushes)], recv_sem=gather_recv.at[slot],
            device_id={"seq": target}, device_id_type=pl.DeviceIdType.MESH,
        )
        copy.start()
        pushes.append(copy)

    def landed(slot):
        pltpu.make_async_remote_copy(
            src_ref=gathered.at[slot], dst_ref=gathered.at[slot],
            send_sem=gather_send.at[0], recv_sem=gather_recv.at[slot],
            device_id={"seq": at(outer, middle, 1 - core)},
            device_id_type=pl.DeviceIdType.MESH,
        ).wait_recv()

    across = at(outer, 1 - middle, core)
    sibling = at(outer, middle, 1 - core)
    for step in range(1, outers):
        push(me, at(outer + step, middle, core))
    push(me, across)
    push(me, sibling)
    for step in range(1, outers):
        slot = at(outer + step, middle, core)
        landed(slot)
        push(slot, across)
        push(slot, sibling)
    for step in range(outers):
        slot = at(outer + step, 1 - middle, core)
        landed(slot)
        push(slot, sibling)
    for step in range(outers):
        landed(at(outer + step, middle, 1 - core))
        landed(at(outer + step, 1 - middle, 1 - core))

    blocks = count // 2
    offset = numbers[2 * blocks]
    first_base = numbers[2 * blocks + 1]
    second_base = numbers[2 * blocks + 2]
    window_start = numbers[2 * blocks + 3]
    pick_row = lax.broadcasted_iota(jnp.int32, (span, 2 * span), 0)
    pick_col = lax.broadcasted_iota(jnp.int32, (span, 2 * span), 1)
    pick = jnp.where(pick_col == pick_row + offset, 1.0, 0.0).astype(jnp.bfloat16)
    key_col = lax.broadcasted_iota(jnp.int32, (span, rows), 1)
    key_pos = jnp.where(key_col < span, first_base + key_col, second_base + key_col - span)
    ahead = key_pos - lax.broadcasted_iota(jnp.int32, (span, rows), 0) - window_start
    lane = lax.broadcasted_iota(jnp.int32, (span, LANES), 1)
    scale = width ** (-0.5)

    def part_copy(target):
        return pltpu.make_async_remote_copy(
            src_ref=parts.at[target], dst_ref=arrived.at[me],
            send_sem=part_send.at[target], recv_sem=part_recv.at[me],
            device_id={"seq": target}, device_id_type=pl.DeviceIdType.MESH,
        )

    def attend(step, carry):
        block = lax.rem(me // 2 + 1 + step, blocks)
        both = jnp.concatenate(
            [gathered[numbers[block]], gathered[numbers[blocks + block]]], axis=0
        )
        queries = jnp.dot(pick, both, preferred_element_type=jnp.float32).astype(jnp.bfloat16)
        allowed = ahead <= block * span
        highs = jnp.zeros((span, LANES), jnp.float32)
        totals = jnp.zeros((span, LANES), jnp.float32)
        for head in range(heads):
            base = head * 3 * width
            keys = projected[:, base + width : base + 2 * width]
            values = projected[:, base + 2 * width : base + 3 * width]
            scores = lax.dot_general(
                queries[:, head * width : (head + 1) * width], keys,
                (((1,), (1,)), ((), ())), preferred_element_type=jnp.float32,
            ) * scale
            scores = jnp.where(allowed, scores, masked_score)
            high = jnp.max(scores, axis=1, keepdims=True)
            weights = jnp.exp(scores - high).astype(jnp.bfloat16)
            total = jnp.sum(weights.astype(jnp.float32), axis=1, keepdims=True)
            summed = jnp.dot(weights, values, preferred_element_type=jnp.float32)
            summed = summed.astype(jnp.bfloat16)
            columns = slice(head * width, (head + 1) * width)
            parts[2 * block, :, columns] = summed[: span // 2]
            parts[2 * block + 1, :, columns] = summed[span // 2 :]
            highs = jnp.where(lane == head, high, highs)
            totals = jnp.where(lane == head, total, totals)
        packed = pack_stats(highs, totals).astype(jnp.bfloat16)
        parts[2 * block, :, total_width:] = packed[: span // 2]
        parts[2 * block + 1, :, total_width:] = packed[span // 2 :]
        for side in range(2):
            target = 2 * block + side

            @pl.when(target != me)
            def _():
                part_copy(target).start()

        return carry

    lax.fori_loop(0, blocks, attend, 0)
    arrived[me] = parts[me]

    def settle(step, carry):
        source = lax.rem(me + step, count)
        pltpu.make_async_remote_copy(
            src_ref=parts.at[source], dst_ref=arrived.at[source],
            send_sem=part_send.at[source], recv_sem=part_recv.at[source],
            device_id={"seq": source}, device_id_type=pl.DeviceIdType.MESH,
        ).wait()
        return carry

    lax.fori_loop(1, count, settle, 0)
    for copy in pushes:
        copy.wait_send()

    def stats_of(source):
        return unpack_stats(arrived[source, :, total_width:].astype(jnp.float32))

    top = lax.fori_loop(
        1, count, lambda source, best: jnp.maximum(best, stats_of(source)[0]), stats_of(0)[0]
    )
    def add(source, carry):
        denominator, pieces = carry
        highs, totals = stats_of(source)
        factor = jnp.exp(highs - top)
        pieces = tuple(
            pieces[head]
            + arrived[source, :, head * width : (head + 1) * width].astype(jnp.float32)
            * factor[:, head : head + 1]
            for head in range(heads)
        )
        return denominator + factor * totals, pieces

    empty = jnp.zeros((span // 2, width), jnp.float32)
    denominator, pieces = lax.fori_loop(
        0, count, add, (jnp.zeros((span // 2, LANES), jnp.float32), (empty,) * heads)
    )
    for head in range(heads):
        context[:, head * width : (head + 1) * width] = (
            pieces[head] / denominator[:, head : head + 1]
        ).astype(jnp.bfloat16)
    top_out[...] = top * width**0.5


def attend_all(numbers, projected, count, heads, width):
    span = projected.shape[0] // 2
    total_width = heads * width
    return pl.pallas_call(
        functools.partial(attend_kernel, count, heads, width),
        out_shape=(
            jax.ShapeDtypeStruct((span // 2, total_width), jnp.bfloat16),
            jax.ShapeDtypeStruct((span // 2, LANES), jnp.float32),
        ),
        in_specs=[
            pl.BlockSpec(memory_space=pltpu.SMEM),
            pl.BlockSpec(memory_space=pltpu.VMEM),
        ],
        out_specs=(
            pl.BlockSpec(memory_space=pltpu.VMEM),
            pl.BlockSpec(memory_space=pltpu.VMEM),
        ),
        scratch_shapes=[
            pltpu.VMEM((count, span, total_width), jnp.bfloat16),
            pltpu.VMEM((count, span // 2, total_width + LANES), jnp.bfloat16),
            pltpu.VMEM((count, span // 2, total_width + LANES), jnp.bfloat16),
            pltpu.SemaphoreType.DMA((count,)),
            pltpu.SemaphoreType.DMA((count,)),
            pltpu.SemaphoreType.DMA((count,)),
            pltpu.SemaphoreType.DMA((count,)),
        ],
        compiler_params=pltpu.CompilerParams(
            collective_id=0, has_side_effects=True, vmem_limit_bytes=40 * 1024 * 1024
        ),
    )(numbers, projected)


def body(byte_rows, pool_weight, norm_gain, qkv_weight, span_order, query_start):
    local_rows, features = byte_rows.shape
    half_rows = local_rows // 2
    short_rows = local_rows // SF
    span_rows = short_rows // 2
    model_width = qkv_weight.shape[0]
    heads_here = qkv_weight.shape[1]
    head_width = qkv_weight.shape[3]
    width_here = heads_here * head_width
    pair_count = lax.axis_size("seq")
    head_count = lax.axis_size("head")
    seq_index = lax.axis_index("seq")
    head_index = lax.axis_index("head")
    pair_slots = jnp.arange(pair_count, dtype=jnp.int32)
    my_pair = jnp.sum(jnp.where(pair_slots == seq_index, span_order, 0))
    shift_rows = SF - 1
    first_tail = byte_rows[half_rows - shift_rows : half_rows]
    last_tail = byte_rows[local_rows - shift_rows :]
    from_before = lax.ppermute(first_tail, "seq", ring(pair_count, 1))
    from_after = lax.ppermute(last_tail, "seq", ring(pair_count, -1))
    first_prev = jnp.where(my_pair == 0, jnp.zeros_like(from_before), from_before)
    second_prev = jnp.where(my_pair == pair_count - 1, first_tail, from_after)
    grouped = jnp.concatenate(
        [
            first_prev,
            byte_rows[: half_rows - shift_rows],
            second_prev,
            byte_rows[half_rows : local_rows - shift_rows],
        ],
        axis=0,
    )
    grouped = grouped.reshape(short_rows, SF * features)
    partial = jnp.dot(
        grouped, pool_weight.reshape(SF * features, model_width), preferred_element_type=jnp.float32
    )
    sent = partial.astype(jnp.bfloat16)
    total = partial
    for step in range(1, head_count):
        total = total + lax.ppermute(sent, "head", ring(head_count, step)).astype(jnp.float32)
    pooled = total.astype(jnp.bfloat16)
    shortened = lax.dynamic_slice_in_dim(pooled, head_index * features, features, 1)
    widened = pooled.astype(jnp.float32)
    squares = jnp.sum(widened * widened, axis=1, keepdims=True) / model_width
    normed = (widened * lax.rsqrt(squares + norm_epsilon) * norm_gain).astype(jnp.bfloat16)
    projected = jnp.dot(
        normed,
        qkv_weight.reshape(model_width, heads_here * 3 * head_width),
        preferred_element_type=jnp.float32,
    ).astype(jnp.bfloat16)
    window_start = query_start[0]
    from_half = window_start - pair_count * span_rows
    blocks = pair_count * QROWS_DEV // span_rows
    places = from_half // span_rows + jnp.arange(blocks, dtype=jnp.int32)
    rotation = span_order[0]
    first_slots = (2 * pair_count - 1 - places - rotation) % pair_count
    second_slots = (2 * pair_count - 2 - places - rotation) % pair_count
    others = jnp.stack(
        [
            from_half % span_rows,
            my_pair * span_rows,
            (2 * pair_count - 1 - my_pair) * span_rows,
            window_start,
        ]
    )
    numbers = jnp.concatenate([first_slots, second_slots, others]).astype(jnp.int32)
    context, top = attend_all(numbers, projected, pair_count, heads_here, head_width)
    return shortened, context, top[:, :heads_here].T


def solution(mesh):
    placed = (P("seq", "head"), P(None, "head", None), P(), P(None, "head", None, None), P(), P())
    return jax.shard_map(
        body,
        mesh=mesh,
        in_specs=placed,
        out_specs=(P("seq", "head"), P("seq", "head"), P("head", "seq")),
        check_vma=False,
    )
```

time: 159 us -> 105 us (0.66)
  the two profiles are of different devices: /device:TPU:11 before, /device:TPU:27 now
where the time goes in v2:
time: 105 us; the launch traced here: 104 us
  Pallas kernels  66.7 us (64%)
  local copies, waits for them, and re-layouts  9.94 us (9%)
  waiting for transfers between devices  9.28 us (9%)
  matrix products  8.02 us (8%)
  between operations  3.99 us (4%)
  other arithmetic  3.91 us (4%)
  starting transfers between devices  2.58 us (2%)
    pallas_call x1, Pallas kernels, attend_all(): pl.pallas_call(functools.partial(attend_kernel, count, heads, width), out...  66.7 us
    ppermute x1, waiting for transfers between devices, body(): lax.ppermute(sent, 'head', ring(head_count, step)).astype(jnp.float32)  6.16 us
    unnamed x9, local copies, waits for them, and re-layouts  5.71 us
    dot_general x1, matrix products, body(): jnp.dot(grouped, pool_weight.reshape(SF * features, model_width), preferr...  5.06 us
    ppermute x1, waiting for transfers between devices, body(): from_after = lax.ppermute(last_tail, 'seq', ring(pair_count, -1))  3.11 us
    dot_general x1, matrix products, body(): jnp.dot(normed, qkv_weight.reshape(model_width, heads_here * 3 * head_wid...  2.96 us
  transfers between devices with their start and end apart: 3, of which 2 were waited for; matrix products, arithmetic and copies ran while one was open for 7% of the time, Pallas kernels for 0%

profile of v2, /device:TPU:27, one launch (start us, length us, event | category | flops | bytes accessed | tf_op | source)
XLA Modules:
  0.0 104.4 jit_solution(15052257641779527523)
XLA Ops:
  0.6 0.7 slice.20
  1.3 0.7 collective-permute-start.1
  2.0 1.3 %fusion.6 = s32[]{:T(128)} fusion(s32[16]{0:T(128)} %param.10, s32[]{:T(128)S(6)} %axis_index.23), kind=kLoop, calls=%fused_computation.21 | loop fusion | flops 47 | bytes 72 | tf_op jit(solution)/shard_map/reduce_sum | solution.py:268
  4.0 3.1 %collective-permute-done.1 = bf16[3,512]{1,0:T(4,128)(2,1)S(1)} collective-permute-done((bf16[3,512]{1,0:T(4,128)(2,1)S(1)}, bf16[3,512]{1,0:T(4,128)(2,1)S(1)}, u32[]{:S(2)}, u32[]{:S(2)}) %collective-permute-start.1) | collective-permute-done | bytes 3104 | tf_op jit(solution)/shard_map/ppermute | solution.py:273
  7.1 0.7 fusion.9
  7.8 0.7 collective-permute-start
  8.4 1.3 %fusion.10 = (bf16[509,512]{1,0:T(8,128)(2,1)S(1)}, bf16[509,512]{1,0:T(8,128)(2,1)S(1)}) fusion(bf16[1024,512]{1,0:T(8,128)(2,1)} %param.6), kind=kLoop, calls=%fused_computation.27 | loop fusion | bytes 2084864 | tf_op jit(solution)/shard_map/slice | solution.py:279
  10.4 0.0 collective-permute-done
  10.4 0.3 pad_maximum_fusion
  10.7 1.5 %reshape.26 = bf16[256,2048]{1,0:T(8,128)(2,1)} reshape(bf16[1024,512]{1,0:T(8,128)(2,1)S(1)} %pad_maximum_fusion) | data formatting | bytes 2097152 | tf_op jit(solution)/shard_map/reshape | solution.py:285
  12.1 0.0 copy-start
  12.1 5.1 %fusion.11 = (bf16[256,1024]{1,0:T(8,128)(2,1)}, f32[256,1024]{1,0:T(8,128)}) fusion(bf16[256,2048]{1,0:T(8,128)(2,1)} %reshape.26, bf16[2048,1024]{1,0:T(8,128)(2,1)} %bitcast.15), kind=kOutput, calls=%fused_computation.28 | convolution fusion | flops 1074003968 | bytes 6815744 | tf_op jit(solution)/shard_map/dot_general | solution.py:286
  17.2 1.2 %collective-permute-start.2 = (bf16[256,1024]{1,0:T(8,128)(2,1)}, bf16[256,1024]{1,0:T(8,128)(2,1)}, u32[]{:S(2)}, u32[]{:S(2)}) collective-permute-start(bf16[256,1024]{1,0:T(8,128)(2,1)} %get-tuple-element.19), channel_id=1, source_target_pairs={{0,1},{1,0},{2,3},{3,2},{4,5},{5,4},{6,7},{7,6},{8,9},{9,8},{10,11... | collective-permute-start | bytes 1572872 | tf_op jit(solution)/shard_map/ppermute | solution.py:292
  20.4 0.0 copy-done
  20.4 0.0 copy-start.1
  20.4 0.0 copy-start.2
  20.4 4.4 %copy.10 = bf16[1024,4,3,128]{0,3,2,1:T(8,128)(2,1)} copy(bf16[1024,4,3,128]{3,1,2,0:T(4,128)(2,1)S(1)} %copy-done) | data formatting | bytes 6291456 | tf_op args[3]
  24.8 0.0 copy-done.1
  24.9 0.1 concatenate.7.numbers
  25.0 6.2 %collective-permute-done.2 = bf16[256,1024]{1,0:T(8,128)(2,1)} collective-permute-done((bf16[256,1024]{1,0:T(8,128)(2,1)}, bf16[256,1024]{1,0:T(8,128)(2,1)}, u32[]{:S(2)}, u32[]{:S(2)}) %collective-permute-start.2) | collective-permute-done | bytes 524320 | tf_op jit(solution)/shard_map/ppermute | solution.py:292
  31.1 1.6 %fusion = (f32[256]{0:T(256)S(1)}, bf16[256,1024]{1,0:T(8,128)(2,1)S(1)}) fusion(f32[256,1024]{1,0:T(8,128)} %get-tuple-element.20, bf16[256,1024]{1,0:T(8,128)(2,1)} %collective-permute-done.2), kind=kLoop, calls=%fused_computation.3 | loop fusion | flops 1572608 | bytes 2098176 | tf_op jit(solution)/shard_map/reduce_sum | solution.py:296
  32.7 0.0 copy-done.2
  32.7 3.0 %convolution_convert_fusion.projected = bf16[256,1536]{1,0:T(8,128)(2,1)S(1)} fusion(bf16[1024,1536]{0,1:T(8,128)(2,1)} %bitcast.13, bf16[256,1024]{1,0:T(8,128)(2,1)S(1)} %get-tuple-element.14, f32[1024]{0:T(1024)S(1)} %copy-done.2, f32[256]{0:T(256)S(1)} %add_rsqrt_fusion), kind=kOutput, calls=%fused_computation | convolution fusion | flops 806748160 | bytes 4461568 | tf_op jit(solution)/shard_map/dot_general | solution.py:298
  35.7 66.7 %shard_map.85 = (bf16[64,512]{1,0:T(8,128)(2,1)S(1)}, f32[64,128]{1,0:T(8,128)S(1)}) custom-call(s32[20]{0:T(128)S(1)} %concatenate.7.numbers, bf16[256,1536]{1,0:T(8,128)(2,1)S(1)} %convolution_convert_fusion.projected), custom_call_target="tpu_custom_call" | custom-call | tf_op jit(solution)/shard_map/pallas_call | solution.py:225
  102.4 0.7 copy.11
  103.0 0.7 constant_dynamic-slice_fusion
  103.8 0.6 copy.14
  (4 shorter events, 0.1 us)
Async XLA Ops:
  1.3 5.7 %collective-permute-start.1 = (bf16[3,512]{1,0:T(4,128)(2,1)S(1)}, bf16[3,512]{1,0:T(4,128)(2,1)S(1)}, u32[]{:S(2)}, u32[]{:S(2)}) collective-permute-start(bf16[3,512]{1,0:T(4,128)(2,1)S(1)} %slice.20), channel_id=1, source_target_pairs={{0,30},{2,0},{4,2},{6,4},{8,6},{10,8},{12,10},{14,12},{16,14},{18,... | collective-permute-start | bytes 9224 | tf_op jit(solution)/shard_map/ppermute | solution.py:273
  7.8 2.6 %collective-permute-start = (bf16[3,512]{1,0:T(4,128)(2,1)S(1)}, bf16[3,512]{1,0:T(4,128)(2,1)S(1)}, u32[]{:S(2)}, u32[]{:S(2)}) collective-permute-start(bf16[3,512]{1,0:T(4,128)(2,1)S(1)} %get-tuple-element.15), channel_id=1, source_target_pairs={{0,2},{2,4},{4,6},{6,8},{8,10},{10,12},{12,14},{14,16},{16,18},{18... | collective-permute-start | bytes 9224 | tf_op jit(solution)/shard_map/ppermute | solution.py:272
  12.1 8.3 %copy-start = (bf16[1024,4,3,128]{3,1,2,0:T(4,128)(2,1)S(1)}, bf16[1024,4,3,128]{3,1,2,0:T(4,128)(2,1)}, u32[]{:S(2)}) copy-start(bf16[1024,4,3,128]{3,1,2,0:T(4,128)(2,1)} %param.9) | copy-start | bytes 9437188
  17.2 14.0 %collective-permute-start.2 = (bf16[256,1024]{1,0:T(8,128)(2,1)}, bf16[256,1024]{1,0:T(8,128)(2,1)}, u32[]{:S(2)}, u32[]{:S(2)}) collective-permute-start(bf16[256,1024]{1,0:T(8,128)(2,1)} %get-tuple-element.19), channel_id=1, source_target_pairs={{0,1},{1,0},{2,3},{3,2},{4,5},{5,4},{6,7},{7,6},{8,9},{9,8},{10,11... | collective-permute-start | bytes 1572872 | tf_op jit(solution)/shard_map/ppermute | solution.py:292
  20.4 4.4 %copy-start.1 = (s32[16]{0:T(128)S(1)}, s32[16]{0:T(128)}, u32[]{:S(2)}) copy-start(s32[16]{0:T(128)} %param.10) | copy-start | bytes 196
  20.4 12.3 %copy-start.2 = (f32[1024]{0:T(1024)S(1)}, f32[1024]{0:T(1024)}, u32[]{:S(2)}) copy-start(f32[1024]{0:T(1024)} %param.8) | copy-start | bytes 12292

commit v3 on v2

--- a/solution.py
+++ b/solution.py
@@ -13,10 +13,6 @@
 
 norm_epsilon = 1e-06
 masked_score = -1e30
-
-
-def ring(count, step):
-    return [(i, (i + step) % count) for i in range(count)]
 
 
 LANES = 128
@@ -44,17 +40,30 @@
 
 
 def attend_kernel(
-    count, heads, width, numbers, projected, context, top_out,
-    gathered, parts, arrived, gather_send, gather_recv, part_send, part_recv,
+    count, head_count, heads, width, numbers, byte_rows, gain, pool_weight, qkv_weight,
+    shortened, context, top_out,
+    tails, pool_held, qkv_held, own, sent, taken, pooled_all, key_values,
+    gathered, parts, arrived,
+    load_sem, tail_send, tail_recv, swap_send, swap_recv,
+    gather_send, gather_recv, part_send, part_recv,
 ):
     me = lax.axis_index("seq")
+    my_head = lax.axis_index("head")
     core = lax.rem(me, 2)
     middle = lax.rem(me // 2, 2)
     outer = me // 4
     outers = count // 4
-    rows = projected.shape[0]
+    rows = key_values.shape[0]
     span = rows // 2
     total_width = heads * width
+    features = byte_rows.shape[1]
+    model_width = pool_held.shape[2]
+    half_rows = SF * span
+    tail_rows = tails.shape[1]
+    pool_load = pltpu.make_async_copy(pool_weight, pool_held, load_sem.at[0])
+    qkv_load = pltpu.make_async_copy(qkv_weight, qkv_held, load_sem.at[1])
+    pool_load.start()
+    qkv_load.start()
 
     def at(outer_at, middle_at, core_at):
         return (lax.rem(outer_at, outers) * 2 + middle_at) * 2 + core_at
@@ -69,11 +78,94 @@
         return carry
 
     lax.fori_loop(1, count, greet, 0)
-    for head in range(heads):
-        gathered[me, :, head * width : (head + 1) * width] = projected[
-            span:, head * 3 * width : (head * 3 + 1) * width
-        ]
-    pl.semaphore_wait(barrier, count - 1)
+    def greet_head(step, carry):
+        pl.semaphore_signal(
+            barrier, inc=1, device_id={"head": lax.rem(my_head + step, head_count)},
+            device_id_type=pl.DeviceIdType.MESH,
+        )
+        return carry
+
+    lax.fori_loop(1, head_count, greet_head, 0)
+    pl.semaphore_wait(barrier, count - 1 + head_count - 1)
+
+    def tail_copy(place, target):
+        end = half_rows * (place + 1)
+        return pltpu.make_async_remote_copy(
+            src_ref=byte_rows.at[end - tail_rows : end], dst_ref=tails.at[place],
+            send_sem=tail_send.at[place], recv_sem=tail_recv.at[place],
+            device_id={"seq": target}, device_id_type=pl.DeviceIdType.MESH,
+        )
+
+    tail_copies = [
+        tail_copy(0, lax.rem(me + 1, count)), tail_copy(1, lax.rem(me + count - 1, count))
+    ]
+    tail_copies[1].start()
+    tail_copies[0].start()
+    pool_row = lax.broadcasted_iota(jnp.int32, (span, half_rows), 0)
+    pool_col = lax.broadcasted_iota(jnp.int32, (span, half_rows), 1)
+    out_row = lax.broadcasted_iota(jnp.int32, (span, features), 0)
+
+    def swap_copy(half, step):
+        target = lax.rem(my_head + step, head_count)
+        return pltpu.make_async_remote_copy(
+            src_ref=sent.at[half], dst_ref=taken.at[my_head, half],
+            send_sem=swap_send.at[step, half], recv_sem=swap_recv.at[my_head, half],
+            device_id={"head": target}, device_id_type=pl.DeviceIdType.MESH,
+        )
+
+    def pool(half, before):
+        block = byte_rows[half * half_rows : (half + 1) * half_rows, :]
+        total = jnp.zeros((span, model_width), jnp.float32)
+        for shift in range(SF):
+            chosen = pool_col == SF * pool_row + (shift - SF + 1)
+            chosen = jnp.where(chosen, 1.0, 0.0).astype(jnp.bfloat16)
+            picked = jnp.dot(chosen, block, preferred_element_type=jnp.float32)
+            if shift < SF - 1:
+                at_row = tail_rows - SF + 1 + shift
+                picked = jnp.where(out_row == 0, before[at_row : at_row + 1], picked)
+            total = total + jnp.dot(
+                picked.astype(jnp.bfloat16), pool_held[shift], preferred_element_type=jnp.float32
+            )
+        own[half] = total
+        sent[half] = total.astype(jnp.bfloat16)
+        for step in range(1, head_count):
+            swap_copy(half, step).start()
+
+    def normed_half(half):
+        total = own[half]
+        for step in range(1, head_count):
+            source = lax.rem(my_head + step, head_count)
+            pltpu.make_async_remote_copy(
+                src_ref=sent.at[half], dst_ref=taken.at[source, half],
+                send_sem=swap_send.at[step, half], recv_sem=swap_recv.at[source, half],
+                device_id={"head": source}, device_id_type=pl.DeviceIdType.MESH,
+            ).wait_recv()
+            total = total + taken[source, half].astype(jnp.float32)
+        pooled = total.astype(jnp.bfloat16)
+        pooled_all[half * span : (half + 1) * span, :] = pooled
+        widened = pooled.astype(jnp.float32)
+        squares = jnp.sum(widened * widened, axis=1, keepdims=True) / model_width
+        return (widened * lax.rsqrt(squares + norm_epsilon) * gain[...]).astype(jnp.bfloat16)
+
+    def project_half(half, normed):
+        key_values[half * span : (half + 1) * span, :] = jnp.dot(
+            normed, qkv_held[:, total_width:], preferred_element_type=jnp.float32
+        ).astype(jnp.bfloat16)
+
+    pair_base = numbers[count + 1]
+    own_tail = byte_rows[half_rows - tail_rows : half_rows, :].astype(jnp.float32)
+    pool_load.wait()
+    tail_copies[1].wait_recv()
+    pool(
+        1, jnp.where(pair_base == (count - 1) * span, own_tail, tails[1].astype(jnp.float32))
+    )
+    tail_copies[0].wait_recv()
+    pool(0, jnp.where(pair_base == 0, 0.0, tails[0].astype(jnp.float32)))
+    qkv_load.wait()
+    late_normed = normed_half(1)
+    gathered[me] = jnp.dot(
+        late_normed, qkv_held[:, :total_width], preferred_element_type=jnp.float32
+    ).astype(jnp.bfloat16)
 
     pushes = []
 
@@ -100,6 +192,11 @@
         push(me, at(outer + step, middle, core))
     push(me, across)
     push(me, sibling)
+    project_half(1, late_normed)
+    project_half(0, normed_half(0))
+    shortened[...] = pooled_all[
+        :, pl.ds(pl.multiple_of(my_head * features, LANES), features)
+    ]
     for step in range(1, outers):
         slot = at(outer + step, middle, core)
         landed(slot)
@@ -144,9 +241,9 @@
         highs = jnp.zeros((span, LANES), jnp.float32)
         totals = jnp.zeros((span, LANES), jnp.float32)
         for head in range(heads):
-            base = head * 3 * width
-            keys = projected[:, base + width : base + 2 * width]
-            values = projected[:, base + 2 * width : base + 3 * width]
+            base = head * width
+            keys = key_values[:, base : base + width]
+            values = key_values[:, total_width + base : total_width + base + width]
             scores = lax.dot_general(
                 queries[:, head * width : (head + 1) * width], keys,
                 (((1,), (1,)), ((), ())), preferred_element_type=jnp.float32,
@@ -189,6 +286,11 @@
     lax.fori_loop(1, count, settle, 0)
     for copy in pushes:
         copy.wait_send()
+    for copy in tail_copies:
+        copy.wait_send()
+    for half in range(2):
+        for step in range(1, head_count):
+            swap_copy(half, step).wait_send()
 
     def stats_of(source):
         return unpack_stats(arrived[source, :, total_width:].astype(jnp.float32))
@@ -219,87 +321,62 @@
     top_out[...] = top * width**0.5
 
 
-def attend_all(numbers, projected, count, heads, width):
-    span = projected.shape[0] // 2
+def whole_kernel(numbers, byte_rows, gain, pool_weight, qkv_weight, count, head_count, heads, width):
+    span = byte_rows.shape[0] // (2 * SF)
+    features = byte_rows.shape[1]
+    model_width = pool_weight.shape[2]
     total_width = heads * width
+    vmem = pl.BlockSpec(memory_space=pltpu.VMEM)
     return pl.pallas_call(
-        functools.partial(attend_kernel, count, heads, width),
+        functools.partial(attend_kernel, count, head_count, heads, width),
         out_shape=(
+            jax.ShapeDtypeStruct((2 * span, features), jnp.bfloat16),
             jax.ShapeDtypeStruct((span // 2, total_width), jnp.bfloat16),
             jax.ShapeDtypeStruct((span // 2, LANES), jnp.float32),
         ),
         in_specs=[
             pl.BlockSpec(memory_space=pltpu.SMEM),
-            pl.BlockSpec(memory_space=pltpu.VMEM),
+            vmem,
+            vmem,
+            pl.BlockSpec(memory_space=pl.ANY),
+            pl.BlockSpec(memory_space=pl.ANY),
         ],
-        out_specs=(
-            pl.BlockSpec(memory_space=pltpu.VMEM),
-            pl.BlockSpec(memory_space=pltpu.VMEM),
-        ),
+        out_specs=(vmem, vmem, vmem),
         scratch_shapes=[
+            pltpu.VMEM((2, 16, features), jnp.bfloat16),
+            pltpu.VMEM(pool_weight.shape, jnp.bfloat16),
+            pltpu.VMEM(qkv_weight.shape, jnp.bfloat16),
+            pltpu.VMEM((2, span, model_width), jnp.float32),
+            pltpu.VMEM((2, span, model_width), jnp.bfloat16),
+            pltpu.VMEM((head_count, 2, span, model_width), jnp.bfloat16),
+            pltpu.VMEM((2 * span, model_width), jnp.bfloat16),
+            pltpu.VMEM((2 * span, 2 * total_width), jnp.bfloat16),
             pltpu.VMEM((count, span, total_width), jnp.bfloat16),
             pltpu.VMEM((count, span // 2, total_width + LANES), jnp.bfloat16),
             pltpu.VMEM((count, span // 2, total_width + LANES), jnp.bfloat16),
+            pltpu.SemaphoreType.DMA((2,)),
+            pltpu.SemaphoreType.DMA((2,)),
+            pltpu.SemaphoreType.DMA((2,)),
+            pltpu.SemaphoreType.DMA((head_count, 2)),
+            pltpu.SemaphoreType.DMA((head_count, 2)),
             pltpu.SemaphoreType.DMA((count,)),
             pltpu.SemaphoreType.DMA((count,)),
             pltpu.SemaphoreType.DMA((count,)),
             pltpu.SemaphoreType.DMA((count,)),
         ],
         compiler_params=pltpu.CompilerParams(
-            collective_id=0, has_side_effects=True, vmem_limit_bytes=40 * 1024 * 1024
+            collective_id=0, has_side_effects=True, vmem_limit_bytes=48 * 1024 * 1024
         ),
-    )(numbers, projected)
+    )(numbers, byte_rows, gain, pool_weight, qkv_weight)
 
 
 def body(byte_rows, pool_weight, norm_gain, qkv_weight, span_order, query_start):
-    local_rows, features = byte_rows.shape
-    half_rows = local_rows // 2
-    short_rows = local_rows // SF
-    span_rows = short_rows // 2
-    model_width = qkv_weight.shape[0]
-    heads_here = qkv_weight.shape[1]
-    head_width = qkv_weight.shape[3]
-    width_here = heads_here * head_width
+    span_rows = byte_rows.shape[0] // (2 * SF)
+    model_width, heads_here, _, head_width = qkv_weight.shape
     pair_count = lax.axis_size("seq")
     head_count = lax.axis_size("head")
-    seq_index = lax.axis_index("seq")
-    head_index = lax.axis_index("head")
     pair_slots = jnp.arange(pair_count, dtype=jnp.int32)
-    my_pair = jnp.sum(jnp.where(pair_slots == seq_index, span_order, 0))
-    shift_rows = SF - 1
-    first_tail = byte_rows[half_rows - shift_rows : half_rows]
-    last_tail = byte_rows[local_rows - shift_rows :]
-    from_before = lax.ppermute(first_tail, "seq", ring(pair_count, 1))
-    from_after = lax.ppermute(last_tail, "seq", ring(pair_count, -1))
-    first_prev = jnp.where(my_pair == 0, jnp.zeros_like(from_before), from_before)
-    second_prev = jnp.where(my_pair == pair_count - 1, first_tail, from_after)
-    grouped = jnp.concatenate(
-        [
-            first_prev,
-            byte_rows[: half_rows - shift_rows],
-            second_prev,
-            byte_rows[half_rows : local_rows - shift_rows],
-        ],
-        axis=0,
-    )
-    grouped = grouped.reshape(short_rows, SF * features)
-    partial = jnp.dot(
-        grouped, pool_weight.reshape(SF * features, model_width), preferred_element_type=jnp.float32
-    )
-    sent = partial.astype(jnp.bfloat16)
-    total = partial
-    for step in range(1, head_count):
-        total = total + lax.ppermute(sent, "head", ring(head_count, step)).astype(jnp.float32)
-    pooled = total.astype(jnp.bfloat16)
-    shortened = lax.dynamic_slice_in_dim(pooled, head_index * features, features, 1)
-    widened = pooled.astype(jnp.float32)
-    squares = jnp.sum(widened * widened, axis=1, keepdims=True) / model_width
-    normed = (widened * lax.rsqrt(squares + norm_epsilon) * norm_gain).astype(jnp.bfloat16)
-    projected = jnp.dot(
-        normed,
-        qkv_weight.reshape(model_width, heads_here * 3 * head_width),
-        preferred_element_type=jnp.float32,
-    ).astype(jnp.bfloat16)
+    my_pair = jnp.sum(jnp.where(pair_slots == lax.axis_index("seq"), span_order, 0))
     window_start = query_start[0]
     from_half = window_start - pair_count * span_rows
     blocks = pair_count * QROWS_DEV // span_rows
@@ -316,7 +393,11 @@
         ]
     )
     numbers = jnp.concatenate([first_slots, second_slots, others]).astype(jnp.int32)
-    context, top = attend_all(numbers, projected, pair_count, heads_here, head_width)
+    qkv_flat = qkv_weight.transpose(0, 2, 1, 3).reshape(model_width, -1)
+    shortened, context, top = whole_kernel(
+        numbers, byte_rows, norm_gain.reshape(1, -1), pool_weight, qkv_flat,
+        pair_count, head_count, heads_here, head_width,
+    )
     return shortened, context, top[:, :heads_here].T
 
 

time: 105 us -> 90.4 us (0.86)
  the two profiles are of different devices: /device:TPU:27 before, /device:TPU:11 now
where the time goes in v3:
time: 90.4 us; the launch traced here: 89.6 us
  Pallas kernels  76.9 us (85%)
  local copies, waits for them, and re-layouts  8.04 us (9%)
  between operations  2.65 us (3%)
  other arithmetic  1.95 us (2%)
    pallas_call x1, Pallas kernels, whole_kernel(): pl.pallas_call(functools.partial(attend_kernel, count, head_count, heads,...  76.9 us
    reshape x1, local copies, waits for them, and re-layouts, body(): qkv_flat = qkv_weight.transpose(0, 2, 1, 3).reshape(model_width, -1)  4.74 us
    unnamed x7, local copies, waits for them, and re-layouts  3.21 us

profile of v3, /device:TPU:11, one launch (start us, length us, event | category | flops | bytes accessed | tf_op | source)
XLA Modules:
  0.0 89.6 jit_solution(6717841793785634897)
XLA Ops:
  1.3 1.3 %fusion = s32[]{:T(128)} fusion(s32[16]{0:T(128)} %param.10, s32[]{:T(128)S(6)} %axis_index.15), kind=kLoop, calls=%fused_computation.8 | loop fusion | flops 47 | bytes 72 | tf_op jit(solution)/shard_map/reduce_sum | solution.py:379
  3.9 0.7 and_select_fusion
  4.6 0.1 concatenate.3.numbers
  4.7 0.0 copy-start.1
  4.7 4.7 %reshape.15.qkv_weight = bf16[1024,1536]{1,0:T(8,128)(2,1)S(1)} reshape(bf16[1024,3,4,128]{3,2,1,0:T(4,128)(2,1)} %bitcast.11) | data formatting | bytes 6291456 | tf_op jit(solution)/shard_map/reshape | solution.py:396
  9.4 0.0 copy-done.1
  9.4 0.0 copy-start
  9.4 1.2 %copy-done = bf16[1024,512]{1,0:T(8,128)(2,1)S(1)} copy-done((bf16[1024,512]{1,0:T(8,128)(2,1)S(1)}, bf16[1024,512]{1,0:T(8,128)(2,1)}, u32[]{:S(2)}) %copy-start) | copy-done | bytes 1048600
  10.6 76.9 %shard_map.85 = (bf16[256,512]{1,0:T(8,128)(2,1)S(1)}, bf16[64,512]{1,0:T(8,128)(2,1)S(1)}, f32[64,128]{1,0:T(8,128)S(1)}) custom-call(s32[20]{0:T(128)S(1)} %concatenate.3.numbers, bf16[1024,512]{1,0:T(8,128)(2,1)S(1)} %copy-done, f32[1,1024]{1,0:T(1,128)S(1)} %bitcast.10, bf16[4,512,1024]{2,1,0:T(8,128)(2,1)} %pool_weight.1, ...), custom_call_target="tpu_custom_call" | custom-call | tf_op jit(solution)/shard_map/pallas_call | solution.py:330
  87.6 0.7 copy.9
  88.3 0.7 copy.13
  89.0 0.6 copy.14
  (1 shorter events, 0.0 us)
Async XLA Ops:
  4.7 4.8 %copy-start.1 = (f32[1024]{0:T(1024)S(1)}, f32[1024]{0:T(1024)}, u32[]{:S(2)}) copy-start(f32[1024]{0:T(1024)} %param.8) | copy-start | bytes 12292
  9.4 1.2 %copy-start = (bf16[1024,512]{1,0:T(8,128)(2,1)S(1)}, bf16[1024,512]{1,0:T(8,128)(2,1)}, u32[]{:S(2)}) copy-start(bf16[1024,512]{1,0:T(8,128)(2,1)} %byte_rows.1) | copy-start | bytes 3145732

commit v4 on v3

--- a/solution.py
+++ b/solution.py
@@ -8,7 +8,6 @@
 from jax.sharding import PartitionSpec as P
 
 SF = 4
-QROWS_DEV = 64
 
 
 norm_epsilon = 1e-06
@@ -40,12 +39,12 @@
 
 
 def attend_kernel(
-    count, head_count, heads, width, numbers, byte_rows, gain, pool_weight, qkv_weight,
+    count, head_count, heads, width, span_order, query_start, byte_rows, gain, pool_weight, qkv_weight,
     shortened, context, top_out,
     tails, pool_held, qkv_held, own, sent, taken, pooled_all, key_values,
-    gathered, parts, arrived,
+    gathered, parts, given, merged, arrived,
     load_sem, tail_send, tail_recv, swap_send, swap_recv,
-    gather_send, gather_recv, part_send, part_recv,
+    gather_send, gather_recv, give_send, give_recv, part_send, part_recv,
 ):
     me = lax.axis_index("seq")
     my_head = lax.axis_index("head")
@@ -152,7 +151,7 @@
             normed, qkv_held[:, total_width:], preferred_element_type=jnp.float32
         ).astype(jnp.bfloat16)
 
-    pair_base = numbers[count + 1]
+    pair_base = span_order[me] * span
     own_tail = byte_rows[half_rows - tail_rows : half_rows, :].astype(jnp.float32)
     pool_load.wait()
     tail_copies[1].wait_recv()
@@ -211,10 +210,14 @@
         landed(at(outer + step, 1 - middle, 1 - core))
 
     blocks = count // 2
-    offset = numbers[2 * blocks]
-    first_base = numbers[2 * blocks + 1]
-    second_base = numbers[2 * blocks + 2]
-    window_start = numbers[2 * blocks + 3]
+    chip = me // 2
+    window_start = query_start[0]
+    from_half = window_start - count * span
+    first_place = lax.div(from_half, span)
+    offset = from_half - first_place * span
+    slot_base = 2 * count - 1 - first_place - span_order[0]
+    first_base = pair_base
+    second_base = (2 * count - 1) * span - pair_base
     pick_row = lax.broadcasted_iota(jnp.int32, (span, 2 * span), 0)
     pick_col = lax.broadcasted_iota(jnp.int32, (span, 2 * span), 1)
     pick = jnp.where(pick_col == pick_row + offset, 1.0, 0.0).astype(jnp.bfloat16)
@@ -224,17 +227,52 @@
     lane = lax.broadcasted_iota(jnp.int32, (span, LANES), 1)
     scale = width ** (-0.5)
 
-    def part_copy(target):
+    half_lane = lax.broadcasted_iota(jnp.int32, (span // 2, LANES), 1)
+
+    def block_at(step):
+        return lax.rem(chip + 1 + step, blocks)
+
+    def give_copy(block):
         return pltpu.make_async_remote_copy(
-            src_ref=parts.at[target], dst_ref=arrived.at[me],
-            send_sem=part_send.at[target], recv_sem=part_recv.at[me],
-            device_id={"seq": target}, device_id_type=pl.DeviceIdType.MESH,
-        )
+            src_ref=parts.at[2 * block + 1 - core], dst_ref=given.at[block],
+            send_sem=give_send.at[block], recv_sem=give_recv.at[block],
+            device_id={"seq": sibling}, device_id_type=pl.DeviceIdType.MESH,
+        )
+
+    def part_copy(block, source):
+        return pltpu.make_async_remote_copy(
+            src_ref=merged.at[block], dst_ref=arrived.at[source],
+            send_sem=part_send.at[block], recv_sem=part_recv.at[source],
+            device_id={"seq": 2 * block + core}, device_id_type=pl.DeviceIdType.MESH,
+        )
+
+    def merge(block, into, place):
+        give_copy(block).wait_recv()
+        mine = 2 * block + core
+        my_highs, my_totals = unpack_stats(parts[mine, :, total_width:].astype(jnp.float32))
+        highs, totals = unpack_stats(given[block, :, total_width:].astype(jnp.float32))
+        best = jnp.maximum(my_highs, highs)
+        my_factor = jnp.exp(my_highs - best)
+        factor = jnp.exp(highs - best)
+        total = my_totals * my_factor + totals * factor
+        for head in range(heads):
+            columns = slice(head * width, (head + 1) * width)
+            into[place, :, columns] = (
+                parts[mine, :, columns].astype(jnp.float32) * my_factor[:, head : head + 1]
+                + given[block, :, columns].astype(jnp.float32) * factor[:, head : head + 1]
+            ).astype(jnp.bfloat16)
+        used = half_lane < heads
+        into[place, :, total_width:] = pack_stats(
+            jnp.where(used, best, 0.0), jnp.where(used, total, 0.0)
+        ).astype(jnp.bfloat16)
 
     def attend(step, carry):
-        block = lax.rem(me // 2 + 1 + step, blocks)
+        block = block_at(step)
         both = jnp.concatenate(
-            [gathered[numbers[block]], gathered[numbers[blocks + block]]], axis=0
+            [
+                gathered[lax.rem(slot_base - block, count)],
+                gathered[lax.rem(slot_base - block - 1, count)],
+            ], axis=0
         )
         queries = jnp.dot(pick, both, preferred_element_type=jnp.float32).astype(jnp.bfloat16)
         allowed = ahead <= block * span
@@ -262,28 +300,32 @@
         packed = pack_stats(highs, totals).astype(jnp.bfloat16)
         parts[2 * block, :, total_width:] = packed[: span // 2]
         parts[2 * block + 1, :, total_width:] = packed[span // 2 :]
-        for side in range(2):
-            target = 2 * block + side
-
-            @pl.when(target != me)
-            def _():
-                part_copy(target).start()
+        give_copy(block).start()
+
+        @pl.when(step > 0)
+        def _():
+            before = block_at(step - 1)
+            merge(before, merged, before)
+            part_copy(before, chip).start()
 
         return carry
 
     lax.fori_loop(0, blocks, attend, 0)
-    arrived[me] = parts[me]
+    merge(chip, arrived, chip)
 
     def settle(step, carry):
-        source = lax.rem(me + step, count)
-        pltpu.make_async_remote_copy(
-            src_ref=parts.at[source], dst_ref=arrived.at[source],
-            send_sem=part_send.at[source], recv_sem=part_recv.at[source],
-            device_id={"seq": source}, device_id_type=pl.DeviceIdType.MESH,
-        ).wait()
+        other = lax.rem(chip + step, blocks)
+        part_copy(other, chip).wait_send()
+        part_copy(other, other).wait_recv()
         return carry
 
-    lax.fori_loop(1, count, settle, 0)
+    lax.fori_loop(1, blocks, settle, 0)
+
+    def given_away(block, carry):
+        give_copy(block).wait_send()
+        return carry
+
+    lax.fori_loop(0, blocks, given_away, 0)
     for copy in pushes:
         copy.wait_send()
     for copy in tail_copies:
@@ -296,7 +338,7 @@
         return unpack_stats(arrived[source, :, total_width:].astype(jnp.float32))
 
     top = lax.fori_loop(
-        1, count, lambda source, best: jnp.maximum(best, stats_of(source)[0]), stats_of(0)[0]
+        1, blocks, lambda source, best: jnp.maximum(best, stats_of(source)[0]), stats_of(0)[0]
     )
     def add(source, carry):
         denominator, pieces = carry
@@ -312,16 +354,19 @@
 
     empty = jnp.zeros((span // 2, width), jnp.float32)
     denominator, pieces = lax.fori_loop(
-        0, count, add, (jnp.zeros((span // 2, LANES), jnp.float32), (empty,) * heads)
+        0, blocks, add, (jnp.zeros((span // 2, LANES), jnp.float32), (empty,) * heads)
     )
     for head in range(heads):
         context[:, head * width : (head + 1) * width] = (
             pieces[head] / denominator[:, head : head + 1]
         ).astype(jnp.bfloat16)
-    top_out[...] = top * width**0.5
-
-
-def whole_kernel(numbers, byte_rows, gain, pool_weight, qkv_weight, count, head_count, heads, width):
+    turned = jnp.concatenate([top, top], axis=0).T
+    top_out[...] = turned[:heads, : span // 2] * width**0.5
+
+
+def whole_kernel(
+    span_order, query_start, byte_rows, gain, pool_weight, qkv_weight, count, head_count, heads, width
+):
     span = byte_rows.shape[0] // (2 * SF)
     features = byte_rows.shape[1]
     model_width = pool_weight.shape[2]
@@ -332,9 +377,10 @@
         out_shape=(
             jax.ShapeDtypeStruct((2 * span, features), jnp.bfloat16),
             jax.ShapeDtypeStruct((span // 2, total_width), jnp.bfloat16),
-            jax.ShapeDtypeStruct((span // 2, LANES), jnp.float32),
+            jax.ShapeDtypeStruct((heads, span // 2), jnp.float32),
         ),
         in_specs=[
+            pl.BlockSpec(memory_space=pltpu.SMEM),
             pl.BlockSpec(memory_space=pltpu.SMEM),
             vmem,
             vmem,
@@ -353,7 +399,9 @@
             pltpu.VMEM((2 * span, 2 * total_width), jnp.bfloat16),
             pltpu.VMEM((count, span, total_width), jnp.bfloat16),
             pltpu.VMEM((count, span // 2, total_width + LANES), jnp.bfloat16),
-            pltpu.VMEM((count, span // 2, total_width + LANES), jnp.bfloat16),
+            pltpu.VMEM((count // 2, span // 2, total_width + LANES), jnp.bfloat16),
+            pltpu.VMEM((count // 2, span // 2, total_width + LANES), jnp.bfloat16),
+            pltpu.VMEM((count // 2, span // 2, total_width + LANES), jnp.bfloat16),
             pltpu.SemaphoreType.DMA((2,)),
             pltpu.SemaphoreType.DMA((2,)),
             pltpu.SemaphoreType.DMA((2,)),
@@ -361,44 +409,24 @@
             pltpu.SemaphoreType.DMA((head_count, 2)),
             pltpu.SemaphoreType.DMA((count,)),
             pltpu.SemaphoreType.DMA((count,)),
-            pltpu.SemaphoreType.DMA((count,)),
-            pltpu.SemaphoreType.DMA((count,)),
+            pltpu.SemaphoreType.DMA((count // 2,)),
+            pltpu.SemaphoreType.DMA((count // 2,)),
+            pltpu.SemaphoreType.DMA((count // 2,)),
+            pltpu.SemaphoreType.DMA((count // 2,)),
         ],
         compiler_params=pltpu.CompilerParams(
             collective_id=0, has_side_effects=True, vmem_limit_bytes=48 * 1024 * 1024
         ),
-    )(numbers, byte_rows, gain, pool_weight, qkv_weight)
+    )(span_order, query_start, byte_rows, gain, pool_weight, qkv_weight)
 
 
 def body(byte_rows, pool_weight, norm_gain, qkv_weight, span_order, query_start):
-    span_rows = byte_rows.shape[0] // (2 * SF)
     model_width, heads_here, _, head_width = qkv_weight.shape
-    pair_count = lax.axis_size("seq")
-    head_count = lax.axis_size("head")
-    pair_slots = jnp.arange(pair_count, dtype=jnp.int32)
-    my_pair = jnp.sum(jnp.where(pair_slots == lax.axis_index("seq"), span_order, 0))
-    window_start = query_start[0]
-    from_half = window_start - pair_count * span_rows
-    blocks = pair_count * QROWS_DEV // span_rows
-    places = from_half // span_rows + jnp.arange(blocks, dtype=jnp.int32)
-    rotation = span_order[0]
-    first_slots = (2 * pair_count - 1 - places - rotation) % pair_count
-    second_slots = (2 * pair_count - 2 - places - rotation) % pair_count
-    others = jnp.stack(
-        [
-            from_half % span_rows,
-            my_pair * span_rows,
-            (2 * pair_count - 1 - my_pair) * span_rows,
-            window_start,
-        ]
+    qkv_flat = qkv_weight.transpose(0, 2, 1, 3).reshape(model_width, -1)
+    return whole_kernel(
+        span_order, query_start, byte_rows, norm_gain.reshape(1, -1), pool_weight, qkv_flat,
+        lax.axis_size("seq"), lax.axis_size("head"), heads_here, head_width,
     )
-    numbers = jnp.concatenate([first_slots, second_slots, others]).astype(jnp.int32)
-    qkv_flat = qkv_weight.transpose(0, 2, 1, 3).reshape(model_width, -1)
-    shortened, context, top = whole_kernel(
-        numbers, byte_rows, norm_gain.reshape(1, -1), pool_weight, qkv_flat,
-        pair_count, head_count, heads_here, head_width,
-    )
-    return shortened, context, top[:, :heads_here].T
 
 
 def solution(mesh):

time: 90.4 us -> 69.1 us (0.76)
  Pallas kernels: 76.9 us -> 58.9 us
  other arithmetic: 1.95 us -> 0 us
  between operations: 2.65 us -> 1.34 us
    pallas_call x1, Pallas kernels: 76.9 us -> 58.9 us  [whole_kernel(): pl.pallas_call(functools.partial(attend_kernel, count, head_count, heads,...]
    reduce_sum x1 -> x0, other arithmetic: 1.29 us -> none  [body(): jnp.sum(jnp.where(pair_slots == lax.axis_index('seq'), span_order, 0))]
    unnamed x7 -> x9, local copies, waits for them, and re-layouts: 3.21 us -> 3.14 us
where the time goes in v4:
time: 69.1 us; the launch traced here: 68.1 us
  Pallas kernels  58.9 us (85%)
  local copies, waits for them, and re-layouts  7.88 us (11%)
  between operations  1.34 us (2%)
    pallas_call x1, Pallas kernels, whole_kernel(): pl.pallas_call(functools.partial(attend_kernel, count, head_count, heads,...  58.9 us
    reshape x1, local copies, waits for them, and re-layouts, body(): qkv_flat = qkv_weight.transpose(0, 2, 1, 3).reshape(model_width, -1)  4.74 us
    unnamed x9, local copies, waits for them, and re-layouts  3.14 us

profile of v4, /device:TPU:11, one launch (start us, length us, event | category | flops | bytes accessed | tf_op | source)
XLA Modules:
  0.0 68.1 jit_solution(9255179769992610869)
XLA Ops:
  1.3 0.0 copy-start.1
  1.3 0.0 copy-start.2
  1.3 4.7 %reshape.13.qkv_weight = bf16[1024,1536]{1,0:T(8,128)(2,1)S(1)} reshape(bf16[1024,3,4,128]{3,2,1,0:T(4,128)(2,1)} %bitcast.3) | data formatting | bytes 6291456 | tf_op jit(solution)/shard_map/reshape | solution.py:425
  6.0 0.0 copy-done.1
  6.1 0.0 copy-done.2
  6.1 0.0 copy-start
  6.1 1.2 %copy-done = bf16[1024,512]{1,0:T(8,128)(2,1)S(1)} copy-done((bf16[1024,512]{1,0:T(8,128)(2,1)S(1)}, bf16[1024,512]{1,0:T(8,128)(2,1)}, u32[]{:S(2)}) %copy-start) | copy-done | bytes 1048600
  7.3 58.9 %shard_map.85 = (bf16[256,512]{1,0:T(8,128)(2,1)S(1)}, bf16[64,512]{1,0:T(8,128)(2,1)S(1)}, f32[4,64]{1,0:T(4,128)S(1)}) custom-call(s32[16]{0:T(128)S(1)} %copy-done.2, s32[1]{0:T(128)S(6)} %copy.12.query_start, bf16[1024,512]{1,0:T(8,128)(2,1)S(1)} %copy-done, f32[1,1024]{1,0:T(1,128)S(1)} %bitcast.2, bf16[4,512,1024]{2,1,0:T(8,128)(2,1)} %pool_weight.1, ...), custom_call_target="tpu_custom_call" | custom-call | tf_op jit(solution)/shard_map/pallas_call | solution.py:375
  66.2 0.7 %copy.13 = bf16[256,512]{1,0:T(8,128)(2,1)} copy(bf16[256,512]{1,0:T(8,128)(2,1)S(1)} %get-tuple-element.6) | data formatting | bytes 524288
  66.9 0.6 copy.14
  67.5 0.6 copy.15
Async XLA Ops:
  1.3 4.8 %copy-start.1 = (f32[1024]{0:T(1024)S(1)}, f32[1024]{0:T(1024)}, u32[]{:S(2)}) copy-start(f32[1024]{0:T(1024)} %param.8) | copy-start | bytes 12292
  1.3 4.8 %copy-start.2 = (s32[16]{0:T(128)S(1)}, s32[16]{0:T(128)}, u32[]{:S(2)}) copy-start(s32[16]{0:T(128)} %span_order.1) | copy-start | bytes 196
  6.1 1.2 %copy-start = (bf16[1024,512]{1,0:T(8,128)(2,1)S(1)}, bf16[1024,512]{1,0:T(8,128)(2,1)}, u32[]{:S(2)}) copy-start(bf16[1024,512]{1,0:T(8,128)(2,1)} %byte_rows.1) | copy-start | bytes 3145732

commit v5 on v4

--- a/solution.py
+++ b/solution.py
@@ -39,9 +39,9 @@
 
 
 def attend_kernel(
-    count, head_count, heads, width, span_order, query_start, byte_rows, gain, pool_weight, qkv_weight,
+    count, head_count, heads, width, span_order, query_start, rows_in, gain, pool_weight, qkv_weight,
     shortened, context, top_out,
-    tails, pool_held, qkv_held, own, sent, taken, pooled_all, key_values,
+    byte_rows, tails, pool_held, qkv_held, own, sent, taken, pooled_all, key_values,
     gathered, parts, given, merged, arrived,
     load_sem, tail_send, tail_recv, swap_send, swap_recv,
     gather_send, gather_recv, give_send, give_recv, part_send, part_recv,
@@ -61,6 +61,8 @@
     tail_rows = tails.shape[1]
     pool_load = pltpu.make_async_copy(pool_weight, pool_held, load_sem.at[0])
     qkv_load = pltpu.make_async_copy(qkv_weight, qkv_held, load_sem.at[1])
+    rows_load = pltpu.make_async_copy(rows_in, byte_rows, load_sem.at[2])
+    rows_load.start()
     pool_load.start()
     qkv_load.start()
 
@@ -85,6 +87,21 @@
         return carry
 
     lax.fori_loop(1, head_count, greet_head, 0)
+    pool_row = lax.broadcasted_iota(jnp.int32, (span, half_rows), 0)
+    pool_col = lax.broadcasted_iota(jnp.int32, (span, half_rows), 1)
+    out_row = lax.broadcasted_iota(jnp.int32, (span, features), 0)
+
+    def pick_rows(half):
+        block = byte_rows[half * half_rows : (half + 1) * half_rows, :]
+        picks = []
+        for shift in range(SF):
+            chosen = pool_col == SF * pool_row + (shift - SF + 1)
+            chosen = jnp.where(chosen, 1.0, 0.0).astype(jnp.bfloat16)
+            picks.append(jnp.dot(chosen, block, preferred_element_type=jnp.float32))
+        return picks
+
+    rows_load.wait()
+    late_picks = pick_rows(1)
     pl.semaphore_wait(barrier, count - 1 + head_count - 1)
 
     def tail_copy(place, target):
@@ -100,10 +117,6 @@
     ]
     tail_copies[1].start()
     tail_copies[0].start()
-    pool_row = lax.broadcasted_iota(jnp.int32, (span, half_rows), 0)
-    pool_col = lax.broadcasted_iota(jnp.int32, (span, half_rows), 1)
-    out_row = lax.broadcasted_iota(jnp.int32, (span, features), 0)
-
     def swap_copy(half, step):
         target = lax.rem(my_head + step, head_count)
         return pltpu.make_async_remote_copy(
@@ -112,13 +125,10 @@
             device_id={"head": target}, device_id_type=pl.DeviceIdType.MESH,
         )
 
-    def pool(half, before):
-        block = byte_rows[half * half_rows : (half + 1) * half_rows, :]
+    def pool(half, picks, before):
         total = jnp.zeros((span, model_width), jnp.float32)
         for shift in range(SF):
-            chosen = pool_col == SF * pool_row + (shift - SF + 1)
-            chosen = jnp.where(chosen, 1.0, 0.0).astype(jnp.bfloat16)
-            picked = jnp.dot(chosen, block, preferred_element_type=jnp.float32)
+            picked = picks[shift]
             if shift < SF - 1:
                 at_row = tail_rows - SF + 1 + shift
                 picked = jnp.where(out_row == 0, before[at_row : at_row + 1], picked)
@@ -153,13 +163,14 @@
 
     pair_base = span_order[me] * span
     own_tail = byte_rows[half_rows - tail_rows : half_rows, :].astype(jnp.float32)
+    early_picks = pick_rows(0)
     pool_load.wait()
     tail_copies[1].wait_recv()
     pool(
-        1, jnp.where(pair_base == (count - 1) * span, own_tail, tails[1].astype(jnp.float32))
+        1, late_picks, jnp.where(pair_base == (count - 1) * span, own_tail, tails[1].astype(jnp.float32))
     )
     tail_copies[0].wait_recv()
-    pool(0, jnp.where(pair_base == 0, 0.0, tails[0].astype(jnp.float32)))
+    pool(0, early_picks, jnp.where(pair_base == 0, 0.0, tails[0].astype(jnp.float32)))
     qkv_load.wait()
     late_normed = normed_half(1)
     gathered[me] = jnp.dot(
@@ -192,15 +203,15 @@
     push(me, across)
     push(me, sibling)
     project_half(1, late_normed)
-    project_half(0, normed_half(0))
-    shortened[...] = pooled_all[
-        :, pl.ds(pl.multiple_of(my_head * features, LANES), features)
-    ]
     for step in range(1, outers):
         slot = at(outer + step, middle, core)
         landed(slot)
         push(slot, across)
         push(slot, sibling)
+    project_half(0, normed_half(0))
+    shortened[...] = pooled_all[
+        :, pl.ds(pl.multiple_of(my_head * features, LANES), features)
+    ]
     for step in range(outers):
         slot = at(outer + step, 1 - middle, core)
         landed(slot)
@@ -382,13 +393,14 @@
         in_specs=[
             pl.BlockSpec(memory_space=pltpu.SMEM),
             pl.BlockSpec(memory_space=pltpu.SMEM),
-            vmem,
+            pl.BlockSpec(memory_space=pl.ANY),
             vmem,
             pl.BlockSpec(memory_space=pl.ANY),
             pl.BlockSpec(memory_space=pl.ANY),
         ],
         out_specs=(vmem, vmem, vmem),
         scratch_shapes=[
+            pltpu.VMEM(byte_rows.shape, jnp.bfloat16),
             pltpu.VMEM((2, 16, features), jnp.bfloat16),
             pltpu.VMEM(pool_weight.shape, jnp.bfloat16),
             pltpu.VMEM(qkv_weight.shape, jnp.bfloat16),
@@ -402,7 +414,7 @@
             pltpu.VMEM((count // 2, span // 2, total_width + LANES), jnp.bfloat16),
             pltpu.VMEM((count // 2, span // 2, total_width + LANES), jnp.bfloat16),
             pltpu.VMEM((count // 2, span // 2, total_width + LANES), jnp.bfloat16),
-            pltpu.SemaphoreType.DMA((2,)),
+            pltpu.SemaphoreType.DMA((3,)),
             pltpu.SemaphoreType.DMA((2,)),
             pltpu.SemaphoreType.DMA((2,)),
             pltpu.SemaphoreType.DMA((head_count, 2)),

time: 69.1 us -> 69.2 us (level)
  no operation moved by 1% of the time
where the time goes in v5:
time: 69.2 us; the launch traced here: 68.2 us
  Pallas kernels  58.9 us (85%)
  local copies, waits for them, and re-layouts  7.88 us (11%)
  between operations  1.34 us (2%)
    pallas_call x1, Pallas kernels, whole_kernel(): pl.pallas_call(functools.partial(attend_kernel, count, head_count, heads,...  58.9 us
    reshape x1, local copies, waits for them, and re-layouts, body(): qkv_flat = qkv_weight.transpose(0, 2, 1, 3).reshape(model_width, -1)  4.74 us
    unnamed x9, local copies, waits for them, and re-layouts  3.14 us

profile of v5, /device:TPU:11, one launch (start us, length us, event | category | flops | bytes accessed | tf_op | source)
XLA Modules:
  0.0 68.2 jit_solution(14967185794824183072)
XLA Ops:
  1.3 0.0 copy-start.1
  1.3 0.0 copy-start.2
  1.3 4.7 %reshape.13.qkv_weight = bf16[1024,1536]{1,0:T(8,128)(2,1)S(1)} reshape(bf16[1024,3,4,128]{3,2,1,0:T(4,128)(2,1)} %bitcast.3) | data formatting | bytes 6291456 | tf_op jit(solution)/shard_map/reshape | solution.py:437
  6.0 0.0 copy-done.1
  6.1 0.0 copy-done.2
  6.1 0.0 copy-start
  6.1 1.2 %copy-done = bf16[1024,512]{1,0:T(8,128)(2,1)S(1)} copy-done((bf16[1024,512]{1,0:T(8,128)(2,1)S(1)}, bf16[1024,512]{1,0:T(8,128)(2,1)}, u32[]{:S(2)}) %copy-start) | copy-done | bytes 1048600
  7.3 58.9 %shard_map.85 = (bf16[256,512]{1,0:T(8,128)(2,1)S(1)}, bf16[64,512]{1,0:T(8,128)(2,1)S(1)}, f32[4,64]{1,0:T(4,128)S(1)}) custom-call(s32[16]{0:T(128)S(1)} %copy-done.2, s32[1]{0:T(128)S(6)} %copy.12.query_start, bf16[1024,512]{1,0:T(8,128)(2,1)S(1)} %copy-done, f32[1,1024]{1,0:T(1,128)S(1)} %bitcast.2, bf16[4,512,1024]{2,1,0:T(8,128)(2,1)} %pool_weight.1, ...), custom_call_target="tpu_custom_call" | custom-call | tf_op jit(solution)/shard_map/pallas_call | solution.py:386
  66.2 0.7 %copy.13 = bf16[256,512]{1,0:T(8,128)(2,1)} copy(bf16[256,512]{1,0:T(8,128)(2,1)S(1)} %get-tuple-element.6) | data formatting | bytes 524288
  66.9 0.6 copy.14
  67.6 0.6 copy.15
Async XLA Ops:
  1.3 4.8 %copy-start.1 = (f32[1024]{0:T(1024)S(1)}, f32[1024]{0:T(1024)}, u32[]{:S(2)}) copy-start(f32[1024]{0:T(1024)} %param.8) | copy-start | bytes 12292
  1.3 4.8 %copy-start.2 = (s32[16]{0:T(128)S(1)}, s32[16]{0:T(128)}, u32[]{:S(2)}) copy-start(s32[16]{0:T(128)} %span_order.1) | copy-start | bytes 196
  6.1 1.2 %copy-start = (bf16[1024,512]{1,0:T(8,128)(2,1)S(1)}, bf16[1024,512]{1,0:T(8,128)(2,1)}, u32[]{:S(2)}) copy-start(bf16[1024,512]{1,0:T(8,128)(2,1)} %rows_in.1) | copy-start | bytes 3145732

commit v6 on v5

--- a/solution.py
+++ b/solution.py
@@ -177,45 +177,76 @@
         late_normed, qkv_held[:, :total_width], preferred_element_type=jnp.float32
     ).astype(jnp.bfloat16)
 
-    pushes = []
-
-    def push(slot, target):
-        copy = pltpu.make_async_remote_copy(
+    across = at(outer, 1 - middle, core)
+    sibling = at(outer, middle, 1 - core)
+    above = at(outer + 1, middle, core)
+    below = at(outer + outers - 1, middle, core)
+
+    def push(slot, kind, target):
+        return pltpu.make_async_remote_copy(
             src_ref=gathered.at[slot], dst_ref=gathered.at[slot],
-            send_sem=gather_send.at[len(pushes)], recv_sem=gather_recv.at[slot],
+            send_sem=gather_send.at[slot, kind], recv_sem=gather_recv.at[slot],
             device_id={"seq": target}, device_id_type=pl.DeviceIdType.MESH,
         )
-        copy.start()
-        pushes.append(copy)
+
+    def spread(slot, up, down, do):
+        if up:
+
+            @pl.when(outer + 1 < outers)
+            def _():
+                do(push(slot, 0, above))
+
+        if down:
+
+            @pl.when(outer > 0)
+            def _():
+                do(push(slot, 1, below))
+
+        do(push(slot, 2, across))
+        do(push(slot, 3, sibling))
+
+    def by_distance(middle_at, do):
+        for step in range(1, outers):
+
+            @pl.when(outer >= step)
+            def _():
+                do(at(outer + outers - step, middle_at, core), True)
+
+            @pl.when(outer + step < outers)
+            def _():
+                do(at(outer + step, middle_at, core), False)
 
     def landed(slot):
         pltpu.make_async_remote_copy(
             src_ref=gathered.at[slot], dst_ref=gathered.at[slot],
-            send_sem=gather_send.at[0], recv_sem=gather_recv.at[slot],
+            send_sem=gather_send.at[slot, 3], recv_sem=gather_recv.at[slot],
             device_id={"seq": at(outer, middle, 1 - core)},
             device_id_type=pl.DeviceIdType.MESH,
         ).wait_recv()
 
-    across = at(outer, 1 - middle, core)
-    sibling = at(outer, middle, 1 - core)
-    for step in range(1, outers):
-        push(me, at(outer + step, middle, core))
-    push(me, across)
-    push(me, sibling)
+    def begin(copy):
+        copy.start()
+
+    def finish(copy):
+        copy.wait_send()
+
+    def pass_along(slot, from_below):
+        landed(slot)
+        spread(slot, from_below, not from_below, begin)
+
+    def pass_over(slot, from_below):
+        landed(slot)
+        push(slot, 3, sibling).start()
+
+    spread(me, True, True, begin)
     project_half(1, late_normed)
-    for step in range(1, outers):
-        slot = at(outer + step, middle, core)
-        landed(slot)
-        push(slot, across)
-        push(slot, sibling)
+    by_distance(middle, pass_along)
     project_half(0, normed_half(0))
     shortened[...] = pooled_all[
         :, pl.ds(pl.multiple_of(my_head * features, LANES), features)
     ]
-    for step in range(outers):
-        slot = at(outer + step, 1 - middle, core)
-        landed(slot)
-        push(slot, sibling)
+    pass_over(across, True)
+    by_distance(1 - middle, pass_over)
     for step in range(outers):
         landed(at(outer + step, middle, 1 - core))
         landed(at(outer + step, 1 - middle, 1 - core))
@@ -337,8 +368,10 @@
         return carry
 
     lax.fori_loop(0, blocks, given_away, 0)
-    for copy in pushes:
-        copy.wait_send()
+    spread(me, True, True, finish)
+    by_distance(middle, lambda slot, from_below: spread(slot, from_below, not from_below, finish))
+    push(across, 3, sibling).wait_send()
+    by_distance(1 - middle, lambda slot, from_below: push(slot, 3, sibling).wait_send())
     for copy in tail_copies:
         copy.wait_send()
     for half in range(2):
@@ -419,7 +452,7 @@
             pltpu.SemaphoreType.DMA((2,)),
             pltpu.SemaphoreType.DMA((head_count, 2)),
             pltpu.SemaphoreType.DMA((head_count, 2)),
-            pltpu.SemaphoreType.DMA((count,)),
+            pltpu.SemaphoreType.DMA((count, 4)),
             pltpu.SemaphoreType.DMA((count,)),
             pltpu.SemaphoreType.DMA((count // 2,)),
             pltpu.SemaphoreType.DMA((count // 2,)),

time: 69.2 us -> 63.9 us (0.923)
  Pallas kernels: 58.9 us -> 54.3 us
    pallas_call x1, Pallas kernels: 58.9 us -> 54.3 us  [whole_kernel(): pl.pallas_call(functools.partial(attend_kernel, count, head_count, heads,...]
where the time goes in v6:
time: 63.9 us; the launch traced here: 63.5 us
  Pallas kernels  54.3 us (85%)
  local copies, waits for them, and re-layouts  7.88 us (12%)
  between operations  1.34 us (2%)
    pallas_call x1, Pallas kernels, whole_kernel(): pl.pallas_call(functools.partial(attend_kernel, count, head_count, heads,...  54.3 us
    reshape x1, local copies, waits for them, and re-layouts, body(): qkv_flat = qkv_weight.transpose(0, 2, 1, 3).reshape(model_width, -1)  4.74 us
    unnamed x9, local copies, waits for them, and re-layouts  3.14 us

profile of v6, /device:TPU:11, one launch (start us, length us, event | category | flops | bytes accessed | tf_op | source)
XLA Modules:
  0.0 63.5 jit_solution(5685375637380452778)
XLA Ops:
  1.3 0.0 copy-start.1
  1.3 0.0 copy-start.2
  1.3 4.7 %reshape.13.qkv_weight = bf16[1024,1536]{1,0:T(8,128)(2,1)S(1)} reshape(bf16[1024,3,4,128]{3,2,1,0:T(4,128)(2,1)} %bitcast.3) | data formatting | bytes 6291456 | tf_op jit(solution)/shard_map/reshape | solution.py:470
  6.0 0.0 copy-done.1
  6.1 0.0 copy-done.2
  6.1 0.0 copy-start
  6.1 1.2 %copy-done = bf16[1024,512]{1,0:T(8,128)(2,1)S(1)} copy-done((bf16[1024,512]{1,0:T(8,128)(2,1)S(1)}, bf16[1024,512]{1,0:T(8,128)(2,1)}, u32[]{:S(2)}) %copy-start) | copy-done | bytes 1048600
  7.3 54.3 %shard_map.85 = (bf16[256,512]{1,0:T(8,128)(2,1)S(1)}, bf16[64,512]{1,0:T(8,128)(2,1)S(1)}, f32[4,64]{1,0:T(4,128)S(1)}) custom-call(s32[16]{0:T(128)S(1)} %copy-done.2, s32[1]{0:T(128)S(6)} %copy.12.query_start, bf16[1024,512]{1,0:T(8,128)(2,1)S(1)} %copy-done, f32[1,1024]{1,0:T(1,128)S(1)} %bitcast.2, bf16[4,512,1024]{2,1,0:T(8,128)(2,1)} %pool_weight.1, ...), custom_call_target="tpu_custom_call" | custom-call | tf_op jit(solution)/shard_map/pallas_call | solution.py:419
  61.6 0.7 %copy.13 = bf16[256,512]{1,0:T(8,128)(2,1)} copy(bf16[256,512]{1,0:T(8,128)(2,1)S(1)} %get-tuple-element.6) | data formatting | bytes 524288
  62.3 0.6 copy.14
  62.9 0.6 copy.15
Async XLA Ops:
  1.3 4.8 %copy-start.1 = (f32[1024]{0:T(1024)S(1)}, f32[1024]{0:T(1024)}, u32[]{:S(2)}) copy-start(f32[1024]{0:T(1024)} %param.8) | copy-start | bytes 12292
  1.3 4.8 %copy-start.2 = (s32[16]{0:T(128)S(1)}, s32[16]{0:T(128)}, u32[]{:S(2)}) copy-start(s32[16]{0:T(128)} %span_order.1) | copy-start | bytes 196
  6.1 1.2 %copy-start = (bf16[1024,512]{1,0:T(8,128)(2,1)S(1)}, bf16[1024,512]{1,0:T(8,128)(2,1)}, u32[]{:S(2)}) copy-start(bf16[1024,512]{1,0:T(8,128)(2,1)} %rows_in.1) | copy-start | bytes 3145732
